TPU v7x, 32 devices: a whole 2x2x4 slice. The times are simulated.
32 devices in a mesh: dp: 8 (over y, x, core), tensor: 4 (over z).
Axes of the slice: x: 2, y: 2, z: 4, core: 2. Of those that a mesh axis runs over, the one named last changes fastest.
Arguments:
- inputs: bfloat16 [16, 1024, 1024], P('dp', 'tensor'), may hold values from -6 to 6
- cotangent: bfloat16 [16, 1024, 1024], P('dp', 'tensor'), may hold values from -6 to 6
- lengths: int32 [16], P('dp'), may hold values from 1 to 1024, as said below
- block_ids: int32 [16, 1024], P('dp'), may hold values from 0 to 7, never falling along the last dimension, each value on 1 to 256 neighbouring positions
- ln1_gain: float32 [1024], replicated, may hold values from 0.5 to 1.5
- ln1_bias: float32 [1024], replicated, may hold values from -1 to 1
- ln2_gain: float32 [1024], replicated, may hold values from 0.5 to 1.5
- ln2_bias: float32 [1024], replicated, may hold values from -1 to 1
- w_qkv: bfloat16 [1024, 3072], P('dp', 'tensor'), may hold values from -0.1875 to 0.1875
- b_qkv: float32 [3072], P('tensor'), may hold values from -1 to 1
- w_out: bfloat16 [1024, 1024], P('dp', 'tensor'), may hold values from -1 to 1
- b_out: float32 [1024], replicated, may hold values from -1 to 1
- w_up: bfloat16 [1024, 4096], P('dp', 'tensor'), may hold values from -0.1875 to 0.1875
- b_up: float32 [4096], P('tensor'), may hold values from -1 to 1
- w_down: bfloat16 [1024, 4096], P('dp', 'tensor'), may hold values from -0.09375 to 0.09375
- b_down: float32 [1024], replicated, may hold values from -1 to 1
Outputs:
- layer_out: bfloat16 [16, 1024, 1024], P('dp', 'tensor')
- grad_inputs: float32 [16, 1024, 1024], P('dp', 'tensor')
- grad_w_qkv: float32 [1024, 3072], P('dp', 'tensor')
- grad_w_out: float32 [1024, 1024], P('dp', 'tensor')
- grad_w_up: float32 [1024, 4096], P('dp', 'tensor')
- grad_w_down: float32 [1024, 4096], P('dp', 'tensor')
- grad_b_qkv: float32 [3072], P('tensor')
- grad_b_up: float32 [4096], P('tensor')
- grad_ln1_gain: float32 [1024], replicated
- grad_ln1_bias: float32 [1024], replicated
- grad_ln2_gain: float32 [1024], replicated
- grad_ln2_bias: float32 [1024], replicated
- grad_b_out: float32 [1024], replicated
- grad_b_down: float32 [1024], replicated
Inputs may be any that keep to these rules, and one draw needn't show every extreme that they name: `lengths`: live tokens of each sequence, at its start; keys from the length on are padding; some sequence has all 1024 live. `block_ids`: along each sequence the block number starts at 0 and never falls; each block spans 1 to 256 consecutive positions and some block spans exactly 256.
All inputs are finite; a program needn't handle non-finite values.
Results may differ from a plain program's by a relative error of at most 0.0098.
Values may be sent and summed in bfloat16 or wider, within the bound.
A program may use at most 256 MiB of HBM per device.

v0:
```python
import jax
import jax.numpy as jnp
from jax import lax
from jax.sharding import PartitionSpec as P

HEAD = 64
ROT = 16
BLOCK = 256
MICRO = 2


def layer_norm(values, ln_gain, ln_bias):
    centre = jnp.mean(values, axis=-1, keepdims=True)
    shifted = values - centre
    spread = jnp.mean(shifted * shifted, axis=-1, keepdims=True)
    return shifted * lax.rsqrt(spread + 1e-05) * ln_gain + ln_bias


def rope_tables(length, rotary):
    halved = rotary // 2
    frequency = 1.0 / 10000.0 ** (jnp.arange(halved, dtype=jnp.float32) * (2.0 / rotary))
    angles = jnp.arange(length, dtype=jnp.float32)[:, None] * frequency[None, :]
    angles = jnp.concatenate([angles, angles], axis=1)[:, None, :]
    return (jnp.cos(angles), jnp.sin(angles))


def rotate(head_rows, cos_table, sin_table, rotary):
    halved = rotary // 2
    moving = head_rows[..., :rotary]
    turned = jnp.concatenate([-moving[..., halved:], moving[..., :halved]], axis=-1)
    moving = moving * cos_table + turned * sin_table
    return jnp.concatenate([moving, head_rows[..., rotary:]], axis=-1)


def visible(block_rows, limits, first_row, tile_rows, key_end):
    own_ids = block_rows[:, first_row : first_row + tile_rows]
    key_pos = jnp.arange(key_end, dtype=jnp.int32)
    allowed = (block_rows[:, None, :key_end] <= own_ids[:, :, None]) & (
        key_pos[None, None, :] < limits[:, None, None]
    )
    return allowed[:, None]


def gelu_exact(argument):
    return jax.nn.gelu(argument, approximate=False)


def on_device(
    inputs,
    cotangent,
    lengths,
    block_ids,
    ln1_gain,
    ln1_bias,
    ln2_gain,
    ln2_bias,
    w_qkv,
    b_qkv,
    w_out,
    b_out,
    w_up,
    b_up,
    w_down,
    b_down,
):
    model_width = inputs.shape[2]
    per_micro = inputs.shape[0] // MICRO
    length = block_ids.shape[1]
    tile_rows = min(512, length)
    heads_here = w_qkv.shape[1] // (3 * HEAD)
    scaling = HEAD ** (-0.5)
    cos_table, sin_table = rope_tables(length, ROT)
    grad_qkv = jnp.zeros((model_width, w_qkv.shape[1]), jnp.float32)
    grad_outw = jnp.zeros((model_width, w_out.shape[1]), jnp.float32)
    grad_upw = jnp.zeros((model_width, w_up.shape[1]), jnp.float32)
    grad_downw = jnp.zeros((model_width, w_down.shape[1]), jnp.float32)
    sum_bias_qkv = jnp.zeros((w_qkv.shape[1],), jnp.float32)
    sum_bias_up = jnp.zeros((w_up.shape[1],), jnp.float32)
    sum_gain_one = jnp.zeros((model_width,), jnp.float32)
    sum_bias_one = jnp.zeros((model_width,), jnp.float32)
    sum_gain_two = jnp.zeros((model_width,), jnp.float32)
    sum_bias_two = jnp.zeros((model_width,), jnp.float32)
    sum_slope = jnp.zeros((model_width,), jnp.float32)
    out_rows = []
    grad_rows = []
    tile_starts = list(range(0, length, tile_rows))
    key_ends = [min(length, first_row + tile_rows + BLOCK) for first_row in tile_starts]
    for micro_idx in range(MICRO):
        first_seq = micro_idx * per_micro
        last_seq = first_seq + per_micro
        residual = inputs[first_seq:last_seq].astype(jnp.float32)
        limits = lengths[first_seq:last_seq]
        block_rows = block_ids[first_seq:last_seq]
        value_one, norm_one_back = jax.vjp(layer_norm, residual, ln1_gain, ln1_bias)
        value_two, norm_two_back = jax.vjp(layer_norm, residual, ln2_gain, ln2_bias)
        whole_one, whole_two = (
            lax.all_gather(value_one.astype(jnp.bfloat16), "tensor", axis=1, tiled=True),
            lax.all_gather(value_two.astype(jnp.bfloat16), "tensor", axis=1, tiled=True),
        )
        qkv_full, out_full, up_full, down_full = (
            lax.all_gather(w_qkv, "dp", axis=0, tiled=True),
            lax.all_gather(w_out, "dp", axis=0, tiled=True),
            lax.all_gather(w_up, "dp", axis=0, tiled=True),
            lax.all_gather(w_down, "dp", axis=0, tiled=True),
        )
        projected = (
            jnp.einsum("bsd,dc->bsc", whole_one, qkv_full, preferred_element_type=jnp.float32)
            + b_qkv
        )
        projected = projected.reshape(per_micro, length, heads_here, 3, HEAD)
        queries = rotate(projected[:, :, :, 0], cos_table, sin_table, ROT).astype(jnp.bfloat16)
        key_rows = rotate(projected[:, :, :, 1], cos_table, sin_table, ROT).astype(jnp.bfloat16)
        values = projected[:, :, :, 2].astype(jnp.bfloat16)
        scaled_q = (queries * jnp.bfloat16(scaling)).transpose(0, 2, 1, 3)
        keys_hd = key_rows.transpose(0, 2, 1, 3)
        values_hd = values.transpose(0, 2, 1, 3)
        log_sums = []
        mixed_parts = []
        for first_row, key_end in zip(tile_starts, key_ends):
            q_block = scaled_q[:, :, first_row : first_row + tile_rows]
            allowed = visible(block_rows, limits, first_row, tile_rows, key_end)
            scores = jnp.einsum(
                "bhqe,bhke->bhqk",
                q_block,
                keys_hd[:, :, :key_end],
                preferred_element_type=jnp.float32,
            )
            scores = jnp.where(allowed, scores, -1e30)
            row_peak = jnp.max(scores, axis=-1)
            powered = jnp.exp(scores - row_peak[..., None])
            totals = jnp.sum(powered, axis=-1)
            soft_low = (powered / totals[..., None]).astype(jnp.bfloat16)
            log_sums.append(row_peak + jnp.log(totals))
            mixed_parts.append(
                jnp.einsum(
                    "bhqk,bhke->bhqe",
                    soft_low,
                    values_hd[:, :, :key_end],
                    preferred_element_type=jnp.float32,
                )
            )
        attended = (
            jnp.concatenate(mixed_parts, axis=2)
            .transpose(0, 2, 1, 3)
            .reshape(per_micro, length, heads_here * HEAD)
            .astype(jnp.bfloat16)
        )
        partial_sum = jnp.einsum(
            "bsf,df->bsd", attended, out_full, preferred_element_type=jnp.float32
        )
        hidden_pre = (
            jnp.einsum("bsd,df->bsf", whole_two, up_full, preferred_element_type=jnp.float32) + b_up
        )
        gelu_value, gelu_back = jax.vjp(gelu_exact, hidden_pre)
        activated = gelu_value.astype(jnp.bfloat16)
        partial_sum = partial_sum + jnp.einsum(
            "bsf,df->bsd", activated, down_full, preferred_element_type=jnp.float32
        )
        reduced = lax.psum_scatter(partial_sum, "tensor", scatter_dimension=1, tiled=True)
        out_rows.append((residual + reduced + b_out + b_down).astype(jnp.bfloat16))
        slope_local = cotangent[first_seq:last_seq]
        slope = lax.all_gather(slope_local, "tensor", axis=1, tiled=True)
        qkv_full, out_full, up_full, down_full = (
            lax.all_gather(w_qkv, "dp", axis=0, tiled=True),
            lax.all_gather(w_out, "dp", axis=0, tiled=True),
            lax.all_gather(w_up, "dp", axis=0, tiled=True),
            lax.all_gather(w_down, "dp", axis=0, tiled=True),
        )
        grad_outw = grad_outw + jnp.einsum(
            "bsd,bsf->df", slope, attended, preferred_element_type=jnp.float32
        )
        grad_downw = grad_downw + jnp.einsum(
            "bsd,bsf->df", slope, activated, preferred_element_type=jnp.float32
        )
        grad_att = jnp.einsum(
            "bsd,df->bsf", slope, out_full, preferred_element_type=jnp.float32
        ).astype(jnp.bfloat16)
        grad_att = grad_att.reshape(per_micro, length, heads_here, HEAD).transpose(0, 2, 1, 3)
        grad_act = jnp.einsum("bsd,df->bsf", slope, down_full, preferred_element_type=jnp.float32)
        grad_hidden = gelu_back(grad_act)[0].astype(jnp.bfloat16)
        grad_upw = grad_upw + jnp.einsum(
            "bsd,bsf->df", whole_two, grad_hidden, preferred_element_type=jnp.float32
        )
        sum_bias_up = sum_bias_up + jnp.sum(grad_hidden.astype(jnp.float32), axis=(0, 1))
        grad_two = jnp.einsum(
            "bsf,df->bsd", grad_hidden, up_full, preferred_element_type=jnp.float32
        )
        grad_keys = jnp.zeros((per_micro, heads_here, length, HEAD), jnp.float32)
        grad_values = jnp.zeros((per_micro, heads_here, length, HEAD), jnp.float32)
        query_parts = []
        for index_tile, first_row in enumerate(tile_starts):
            key_end = key_ends[index_tile]
            q_block = scaled_q[:, :, first_row : first_row + tile_rows]
            g_block = grad_att[:, :, first_row : first_row + tile_rows]
            k_block = keys_hd[:, :, :key_end]
            allowed = visible(block_rows, limits, first_row, tile_rows, key_end)
            scores = jnp.einsum(
                "bhqe,bhke->bhqk", q_block, k_block, preferred_element_type=jnp.float32
            )
            scores = jnp.where(allowed, scores, -1e30)
            soft_full = jnp.exp(scores - log_sums[index_tile][..., None])
            soft_low = soft_full.astype(jnp.bfloat16)
            value_part = jnp.einsum(
                "bhqk,bhqe->bhke", soft_low, g_block, preferred_element_type=jnp.float32
            )
            grad_values = grad_values.at[:, :, :key_end].add(value_part)
            grad_soft = jnp.einsum(
                "bhqe,bhke->bhqk",
                g_block,
                values_hd[:, :, :key_end],
                preferred_element_type=jnp.float32,
            )
            centred = jnp.sum(soft_full * grad_soft, axis=-1)
            grad_scores = (soft_full * (grad_soft - centred[..., None])).astype(jnp.bfloat16)
            query_parts.append(
                jnp.einsum(
                    "bhqk,bhke->bhqe", grad_scores, k_block, preferred_element_type=jnp.float32
                )
                * scaling
            )
            key_part = jnp.einsum(
                "bhqk,bhqe->bhke", grad_scores, q_block, preferred_element_type=jnp.float32
            )
            grad_keys = grad_keys.at[:, :, :key_end].add(key_part)
        grad_queries = jnp.concatenate(query_parts, axis=2).transpose(0, 2, 1, 3)
        grad_keys = grad_keys.transpose(0, 2, 1, 3)
        grad_values = grad_values.transpose(0, 2, 1, 3)
        grad_projected = jnp.stack(
            [
                rotate(grad_queries, cos_table, -sin_table, ROT),
                rotate(grad_keys, cos_table, -sin_table, ROT),
                grad_values,
            ],
            axis=3,
        )
        grad_projected = grad_projected.reshape(per_micro, length, 3 * heads_here * HEAD).astype(
            jnp.bfloat16
        )
        grad_qkv = grad_qkv + jnp.einsum(
            "bsd,bsc->dc", whole_one, grad_projected, preferred_element_type=jnp.float32
        )
        sum_bias_qkv = sum_bias_qkv + jnp.sum(grad_projected.astype(jnp.float32), axis=(0, 1))
        grad_one = jnp.einsum(
            "bsc,dc->bsd", grad_projected, qkv_full, preferred_element_type=jnp.float32
        )
        slope_rows = slope_local.astype(jnp.float32)
        back_one, back_two = (
            lax.psum_scatter(grad_one, "tensor", scatter_dimension=1, tiled=True),
            lax.psum_scatter(grad_two, "tensor", scatter_dimension=1, tiled=True),
        )
        input_one, gain_one, bias_one = norm_one_back(back_one)
        input_two, gain_two, bias_two = norm_two_back(back_two)
        grad_rows.append(slope_rows + input_one + input_two)
        sum_gain_one = sum_gain_one + gain_one
        sum_bias_one = sum_bias_one + bias_one
        sum_gain_two = sum_gain_two + gain_two
        sum_bias_two = sum_bias_two + bias_two
        sum_slope = sum_slope + jnp.sum(slope_rows, axis=(0, 1))
    reduced_grads = (
        lax.psum_scatter(grad_qkv, "dp", scatter_dimension=0, tiled=True),
        lax.psum_scatter(grad_outw, "dp", scatter_dimension=0, tiled=True),
        lax.psum_scatter(grad_upw, "dp", scatter_dimension=0, tiled=True),
        lax.psum_scatter(grad_downw, "dp", scatter_dimension=0, tiled=True),
    )
    bias_qkv_total, bias_up_total = lax.psum((sum_bias_qkv, sum_bias_up), "dp")
    shared = lax.psum(
        (sum_gain_one, sum_bias_one, sum_gain_two, sum_bias_two, sum_slope), ("dp", "tensor")
    )
    return (
        jnp.concatenate(out_rows, axis=0),
        jnp.concatenate(grad_rows, axis=0),
        reduced_grads[0],
        reduced_grads[1],
        reduced_grads[2],
        reduced_grads[3],
        bias_qkv_total,
        bias_up_total,
        shared[0],
        shared[1],
        shared[2],
        shared[3],
        shared[4],
        shared[4],
    )


def solution(mesh):
    in_specs = (
        P("dp", "tensor", None),
        P("dp", "tensor", None),
        P("dp"),
        P("dp", None),
        P(),
        P(),
        P(),
        P(),
        P("dp", "tensor"),
        P("tensor"),
        P("dp", "tensor"),
        P(),
        P("dp", "tensor"),
        P("tensor"),
        P("dp", "tensor"),
        P(),
    )
    out_specs = (
        P("dp", "tensor", None),
        P("dp", "tensor", None),
        P("dp", "tensor"),
        P("dp", "tensor"),
        P("dp", "tensor"),
        P("dp", "tensor"),
        P("tensor"),
        P("tensor"),
        P(),
        P(),
        P(),
        P(),
        P(),
        P(),
    )
    return jax.shard_map(
        on_device, mesh=mesh, in_specs=in_specs, out_specs=out_specs, check_vma=False
    )
```

profile of v0, /device:TPU:0, one launch (start us, length us, event | category | flops | bytes accessed | tf_op | source)
XLA Modules:
  0.0 1063.5 jit_solution(9621609152329100266)
XLA Ops:
  11.7 3.2 fusion.173
  24.5 12.7 %all_gather.44 = bf16[1024,256]{1,0:T(8,128)(2,1)S(1)} all-gather(bf16[128,256]{1,0:T(8,128)(2,1)S(1)} %copy-done.88), channel_id=1, replica_groups=mesh['dp'=8,'tensor'=4] {'dp'}, dimensions={0}, use_global_device_ids=true | all-gather | bytes 589824 | tf_op jit(solution)/shard_map/all_gather | solution.py:102
  39.7 48.1 %all-gather.10.cloned.1.call-done = bf16[1,1024,1024]{2,1,0:T(8,128)(2,1)} async-done(((bf16[1,256,1024]{2,1,0:T(8,128)(2,1)}), bf16[1,1024,1024]{2,1,0:T(8,128)(2,1)}) %all-gather.10.cloned.1.call-update) | async-done | bytes 2097168 | tf_op jit(solution)/shard_map/all_gather | solution.py:97
  87.8 3.9 fusion.85
  96.9 37.2 %all-gather.20.cloned.1.call-done = bf16[1,1024,1024]{2,1,0:T(8,128)(2,1)} async-done(((bf16[1,256,1024]{2,1,0:T(8,128)(2,1)}), bf16[1,1024,1024]{2,1,0:T(8,128)(2,1)}) %all-gather.20.cloned.1.call-update) | async-done | bytes 2097168 | tf_op jit(solution)/shard_map/all_gather | solution.py:97
  134.1 3.9 fusion.91
  147.8 2.8 fusion.161
  150.5 29.7 %all-gather.24.cloned.1.call-done = bf16[1,1024,1024]{2,1,0:T(8,128)(2,1)} async-done(((bf16[1,256,1024]{2,1,0:T(8,128)(2,1)}), bf16[1,1024,1024]{2,1,0:T(8,128)(2,1)}) %all-gather.24.cloned.1.call-update) | async-done | bytes 2097168 | tf_op jit(solution)/shard_map/all_gather | solution.py:162
  180.2 2.3 fusion.142
  182.6 4.8 multiply_reduce_fusion.3
  194.4 2.2 fusion
  197.7 3.6 fusion.155
  202.8 2.1 fusion.3
  205.0 2.0 fusion.160
  208.6 2.3 fusion.1
  212.0 3.8 fusion.154
  215.9 10.4 all-gather.26.cloned.1.call-done
  226.3 3.3 fusion.145
  229.6 2.4 fusion.46
  234.4 6.3 multiply_reduce_fusion.1
  240.8 2.3 multiply_convert_fusion.1
  243.2 2.2 fusion.158
  247.4 2.6 multiply_reduce_fusion.2
  251.7 21.3 %all-gather.22.cloned.1.call-done = bf16[1,1024,1024]{2,1,0:T(8,128)(2,1)} async-done(((bf16[1,256,1024]{2,1,0:T(8,128)(2,1)}), bf16[1,1024,1024]{2,1,0:T(8,128)(2,1)}) %all-gather.22.cloned.1.call-update) | async-done | bytes 2097168 | tf_op jit(solution)/shard_map/all_gather | solution.py:98
  273.0 28.5 %all-gather.16.cloned.1.call-done = bf16[1024,1024]{1,0:T(8,128)(2,1)} async-done(((bf16[128,1024]{1,0:T(8,128)(2,1)}), bf16[1024,1024]{1,0:T(8,128)(2,1)}) %all-gather.16.cloned.1.call-update) | async-done | bytes 2097168 | tf_op jit(solution)/shard_map/all_gather | solution.py:103
  301.5 6.6 fusion.66
  308.2 41.5 %all-gather.14.cloned.1.call-done = bf16[1,1024,1024]{2,1,0:T(8,128)(2,1)} async-done(((bf16[1,256,1024]{2,1,0:T(8,128)(2,1)}), bf16[1,1024,1024]{2,1,0:T(8,128)(2,1)}) %all-gather.14.cloned.1.call-update) | async-done | bytes 2097168 | tf_op jit(solution)/shard_map/all_gather | solution.py:98
  349.6 23.9 %multiply_convert_fusion.5 = (bf16[1024,1024]{1,0:T(8,128)(2,1)S(1)}, f32[1024,1024]{1,0:T(8,128)}, bf16[1024,1024]{1,0:T(8,128)(2,1)S(1)}, f32[1024,1024]{1,0:T(8,128)}, f32[1024,1024]{1,0:T(8,128)}) fusion(f32[1024]{0:T(1024)} %param.53, f32[1024,1024]{1,0:T(8,128)} %fusion.66, bf16[1024,1024]{1,0:T(8,128)(2,1)} %all-gather.16.cloned.1.call-done, ...), kind=kOutput, calls=%fused_computation.58 | convolution fusion | flops 2285895680 | bytes 25169920 | tf_op jit(solution)/shard_map/bsd,df->bsf/dot_general | solution.py:152
  373.6 2.4 fusion.44
  376.7 4.5 add_bitcast_fusion
  385.4 3.0 fusion.156
  388.4 6.6 multiply_reduce_fusion
  395.1 2.1 multiply_convert_fusion
  405.4 2.2 fusion.139
  409.1 3.9 convolution_bitcast_fusion.1
  414.7 4.4 fusion.151
  419.1 4.7 fusion.133
  425.5 3.9 convolution_bitcast_fusion
  431.1 7.4 convert_reduce_fusion
  439.9 4.4 convolution_bitcast_fusion.2
  445.9 6.8 convert_reduce_fusion.1
  454.2 4.5 convolution_bitcast_fusion.3
  460.2 4.0 fusion.252
  464.2 2.7 add_bitcast_fusion.1
  467.0 4.1 fusion.251
  471.1 2.8 add_bitcast_fusion.2
  475.3 3.6 fusion.68
  478.9 3.6 fusion.88
  482.6 4.8 fusion.64
  487.4 4.5 fusion.80
  492.2 16.0 %all-reduce.5 = (f32[768]{0:T(1024)}, f32[1024]{0:T(1024)}) all-reduce(f32[768]{0:T(1024)S(1)} %add.401, f32[1024]{0:T(1024)S(1)} %add.402), channel_id=1, replica_groups=mesh['dp'=8,'tensor'=4] {'dp'}, use_global_device_ids=true, to_apply=%region_36.37 | all-reduce | flops 1792 | bytes 14336 | tf_op jit(solution)/shard_map/psum | solution.py:265
  509.8 2.0 copy.58
  511.8 39.2 %reduce-scatter.15.cloned.1.call-done = f32[1,256,1024]{2,1,0:T(8,128)} async-done(((f32[1,1024,1024]{2,1,0:T(8,128)}), f32[1,256,1024]{2,1,0:T(8,128)}) %reduce-scatter.15.cloned.1.call-update) | async-done | bytes 1048592 | tf_op jit(solution)/shard_map/reduce_scatter | solution.py:248
  551.1 79.6 %reduce-scatter.19.cloned.1.call-done = f32[1,256,1024]{2,1,0:T(8,128)} async-done(((f32[1,1024,1024]{2,1,0:T(8,128)}), f32[1,256,1024]{2,1,0:T(8,128)}) %reduce-scatter.19.cloned.1.call-update) | async-done | bytes 1048592 | tf_op jit(solution)/shard_map/reduce_scatter | solution.py:248
  630.6 2.0 fusion.177
  632.7 77.5 %reduce-scatter.21.cloned.1.call-done = f32[1,256,1024]{2,1,0:T(8,128)} async-done(((f32[1,1024,1024]{2,1,0:T(8,128)}), f32[1,256,1024]{2,1,0:T(8,128)}) %reduce-scatter.21.cloned.1.call-update) | async-done | bytes 1048592 | tf_op jit(solution)/shard_map/reduce_scatter | solution.py:249
  710.2 79.4 %reduce-scatter.17.cloned.1.call-done = f32[1,256,1024]{2,1,0:T(8,128)} async-done(((f32[1,1024,1024]{2,1,0:T(8,128)}), f32[1,256,1024]{2,1,0:T(8,128)}) %reduce-scatter.17.cloned.1.call-update) | async-done | bytes 1048592 | tf_op jit(solution)/shard_map/reduce_scatter | solution.py:249
  789.7 3.2 fusion.178
  795.8 44.0 %all-reduce.4 = (f32[1024]{0:T(1024)}, f32[1024]{0:T(1024)}, f32[1024]{0:T(1024)}, f32[1024]{0:T(1024)}, f32[1024]{0:T(1024)S(1)}) all-reduce(f32[1024]{0:T(1024)S(1)} %add.403, f32[1024]{0:T(1024)S(1)} %add.404, f32[1024]{0:T(1024)S(1)} %add.405, f32[1024]{0:T(1024)S(1)} %add.406, ...), channel_id=1, replica_groups=mesh['dp'=8,'tensor'=4] {'dp','tensor'}, use_global_device_ids=true, to_apply=%region_42.43 | all-reduce | flops 5120 | bytes 40960 | tf_op jit(solution)/shard_map/psum | solution.py:266
  839.8 30.5 %reduce-scatter.13.cloned.1.call-done = f32[1,256,1024]{2,1,0:T(8,128)} async-done(((f32[1,1024,1024]{2,1,0:T(8,128)}), f32[1,256,1024]{2,1,0:T(8,128)}) %reduce-scatter.13.cloned.1.call-update) | async-done | bytes 1048592 | tf_op jit(solution)/shard_map/reduce_scatter | solution.py:159
  870.2 79.4 %reduce-scatter.11.cloned.1.call-done = f32[1,256,1024]{2,1,0:T(8,128)} async-done(((f32[1,1024,1024]{2,1,0:T(8,128)}), f32[1,256,1024]{2,1,0:T(8,128)}) %reduce-scatter.11.cloned.1.call-update) | async-done | bytes 1048592 | tf_op jit(solution)/shard_map/reduce_scatter | solution.py:159
  949.6 2.7 fusion.181
  954.9 45.7 %reduce-scatter.23.cloned.1.call-done = f32[128,768]{1,0:T(8,128)} async-done(((f32[1024,768]{1,0:T(8,128)}), f32[128,768]{1,0:T(8,128)}) %reduce-scatter.23.cloned.1.call-update) | async-done | bytes 393232 | tf_op jit(solution)/shard_map/reduce_scatter | solution.py:260
  1000.6 55.3 %reduce-scatter.27.cloned.1.call-done = f32[128,1024]{1,0:T(8,128)} async-done(((f32[1024,1024]{1,0:T(8,128)}), f32[128,1024]{1,0:T(8,128)}) %reduce-scatter.27.cloned.1.call-update) | async-done | bytes 524304 | tf_op jit(solution)/shard_map/reduce_scatter | solution.py:262
  (415 shorter events, 83.8 us)
Async XLA Ops:
  7.2 8.5 copy-start.16
  7.2 32.6 %all-gather.12.cloned.1.call-start = ((), (), s32[]{:S(2)}) async-start(), calls=%async_computation.11 | async-start | bytes 1769472 | tf_op jit(solution)/shard_map/all_gather | solution.py:101
  7.9 79.9 %all-gather.10.cloned.1.call-start = ((), (), s32[]{:S(2)}) async-start(), calls=%async_computation.10 | async-start | bytes 2621440 | tf_op jit(solution)/shard_map/all_gather | solution.py:97
  9.4 5.4 copy-start.92
  11.6 8.6 copy-start.105
  11.7 11.8 %copy-start.89 = (s32[2,1024]{1,0:T(2,128)S(1)}, s32[2,1024]{1,0:T(2,128)}, u32[]{:S(2)}) copy-start(s32[2,1024]{1,0:T(2,128)} %param.43) | copy-start | bytes 24580
  11.7 12.8 %copy-start.88 = (bf16[128,256]{1,0:T(8,128)(2,1)S(1)}, bf16[128,256]{1,0:T(8,128)(2,1)}, u32[]{:S(2)}) copy-start(bf16[128,256]{1,0:T(8,128)(2,1)} %param.50) | copy-start | bytes 196612
  14.8 73.0 %copy-start.113 = (f32[768]{0:T(1024)S(1)}, f32[768]{0:T(1024)}, u32[]{:S(2)}) copy-start(f32[768]{0:T(1024)} %param.49) | copy-start | bytes 9220
  14.9 119.2 %all-gather.20.cloned.1.call-start = ((), (), s32[]{:S(2)}) async-start(), calls=%async_computation.16 | async-start | bytes 2621440 | tf_op jit(solution)/shard_map/all_gather | solution.py:97
  15.6 164.6 %all-gather.24.cloned.1.call-start = ((), (), s32[]{:S(2)}) async-start(), calls=%async_computation.19 | async-start | bytes 2621440 | tf_op jit(solution)/shard_map/all_gather | solution.py:162
  16.8 209.5 %all-gather.26.cloned.1.call-start = ((), (), s32[]{:S(2)}) async-start(), calls=%async_computation.22 | async-start | bytes 2621440 | tf_op jit(solution)/shard_map/all_gather | solution.py:162
  17.4 255.6 %all-gather.22.cloned.1.call-start = ((), (), s32[]{:S(2)}) async-start(), calls=%async_computation.17 | async-start | bytes 2621440 | tf_op jit(solution)/shard_map/all_gather | solution.py:98
  18.0 283.6 %all-gather.16.cloned.1.call-start = ((), (), s32[]{:S(2)}) async-start(), calls=%async_computation.13 | async-start | bytes 2359296 | tf_op jit(solution)/shard_map/all_gather | solution.py:103
  18.7 330.9 %all-gather.14.cloned.1.call-start = ((), (), s32[]{:S(2)}) async-start(), calls=%async_computation.12 | async-start | bytes 2621440 | tf_op jit(solution)/shard_map/all_gather | solution.py:98
  19.5 410.0 %all-gather.18.cloned.1.call-start = ((), (), s32[]{:S(2)}) async-start(), calls=%async_computation.14 | async-start | bytes 2359296 | tf_op jit(solution)/shard_map/all_gather | solution.py:104
  20.2 487.9 %reduce-scatter.25.cloned.1.call-start = ((), (), s32[]{:S(2)}) async-start(), calls=%async_computation.26 | async-start | bytes 1179648 | tf_op jit(solution)/shard_map/reduce_scatter | solution.py:261
  37.2 189.1 %copy-start.21 = (bf16[1024,256]{1,0:T(8,128)(2,1)}, bf16[1024,256]{1,0:T(8,128)(2,1)S(1)}, u32[]{:S(2)}) copy-start(bf16[1024,256]{1,0:T(8,128)(2,1)S(1)} %all_gather.44) | copy-start | bytes 1572868
  37.6 173.3 %copy-start.7 = (pred[512,1024]{1,0:T(8,128)(4,1)}, pred[512,1024]{1,0:T(8,128)(4,1)S(1)}, u32[]{:S(2)}) copy-start(pred[512,1024]{1,0:T(8,128)(4,1)S(1)} %compare_and_fusion) | copy-start | bytes 1572868
  38.0 202.7 %copy-start.10 = (pred[512,1024]{1,0:T(8,128)(4,1)}, pred[512,1024]{1,0:T(8,128)(4,1)S(1)}, u32[]{:S(2)}) copy-start(pred[512,1024]{1,0:T(8,128)(4,1)S(1)} %compare_and_fusion.1) | copy-start | bytes 1572868
  38.6 148.7 %copy-start.5 = (pred[512,768]{1,0:T(8,128)(4,1)}, pred[512,768]{1,0:T(8,128)(4,1)S(1)}, u32[]{:S(2)}) copy-start(pred[512,768]{1,0:T(8,128)(4,1)S(1)} %get-tuple-element.314) | copy-start | bytes 1179652
  143.6 49.2 %copy-start.60 = (bf16[1,1024,4,16]{1,3,2,0:T(8,128)(2,1)}, bf16[1,1024,4,16]{1,3,2,0:T(8,128)(2,1)S(1)}, u32[]{:S(2)}) copy-start(bf16[1,1024,4,16]{1,3,2,0:T(8,128)(2,1)S(1)} %get-tuple-element.271) | copy-start | bytes 393220
  143.6 63.4 %copy-start.58 = (bf16[1,1024,4,16]{1,3,2,0:T(8,128)(2,1)}, bf16[1,1024,4,16]{1,3,2,0:T(8,128)(2,1)S(1)}, u32[]{:S(2)}) copy-start(bf16[1,1024,4,16]{1,3,2,0:T(8,128)(2,1)S(1)} %get-tuple-element.273) | copy-start | bytes 393220
  147.8 39.6 %copy-start.80 = (f32[4,512]{1,0:T(4,128)}, f32[4,512]{1,0:T(4,128)S(1)}, u32[]{:S(2)}) copy-start(f32[4,512]{1,0:T(4,128)S(1)} %log_add_fusion.3) | copy-start | bytes 24580
  182.6 5.2 slice-start.1
  201.5 5.5 copy-start.19
  215.9 17.9 %copy-start.23 = (bf16[1,4,1024,64]{2,3,1,0:T(8,128)(2,1)}, bf16[1,4,1024,64]{2,3,1,0:T(8,128)(2,1)S(1)}, u32[]{:S(2)}) copy-start(bf16[1,4,1024,64]{2,3,1,0:T(8,128)(2,1)S(1)} %maximum_convert_fusion.2) | copy-start | bytes 1572868
  215.9 17.9 %copy-start.25 = (bf16[1,4,1024,64]{2,3,1,0:T(8,128)(2,1)}, bf16[1,4,1024,64]{2,3,1,0:T(8,128)(2,1)S(1)}, u32[]{:S(2)}) copy-start(bf16[1,4,1024,64]{2,3,1,0:T(8,128)(2,1)S(1)} %maximum_convert_fusion.3) | copy-start | bytes 1572868
  226.3 5.7 copy-start.43
  233.8 7.0 slice-start.8
  234.4 6.4 slice-start.9
  251.6 258.2 %reduce-scatter.29.cloned.1.call-start = ((), (), s32[]{:S(2)}) async-start(), calls=%async_computation.28 | async-start | bytes 4718592 | tf_op jit(solution)/shard_map/reduce_scatter | solution.py:263
  349.6 23.9 %copy-start.41 = (bf16[1,1024,1024]{2,1,0:T(8,128)(2,1)S(1)}, bf16[1,1024,1024]{2,1,0:T(8,128)(2,1)}, u32[]{:S(2)}) copy-start(bf16[1,1024,1024]{2,1,0:T(8,128)(2,1)} %all-gather.26.cloned.1.call-done) | copy-start | bytes 6291460
  381.2 169.8 %reduce-scatter.15.cloned.1.call-start = ((), (), s32[]{:S(2)}) async-start(), calls=%async_computation.20 | async-start | bytes 5242880 | tf_op jit(solution)/shard_map/reduce_scatter | solution.py:248
  381.3 7.1 copy-start.8
  381.3 7.1 copy-start.66
  381.3 7.1 copy-start.84
  385.4 9.6 slice-start.6
  388.4 6.6 slice-start.7
  408.1 5.0 copy-start.50
  413.1 217.5 %reduce-scatter.19.cloned.1.call-start = ((), (), s32[]{:S(2)}) async-start(), calls=%async_computation.23 | async-start | bytes 5242880 | tf_op jit(solution)/shard_map/reduce_scatter | solution.py:248
  429.4 280.8 %reduce-scatter.21.cloned.1.call-start = ((), (), s32[]{:S(2)}) async-start(), calls=%async_computation.24 | async-start | bytes 5242880 | tf_op jit(solution)/shard_map/reduce_scatter | solution.py:249
  431.1 8.7 copy-start.109
  444.3 345.3 %reduce-scatter.17.cloned.1.call-start = ((), (), s32[]{:S(2)}) async-start(), calls=%async_computation.21 | async-start | bytes 5242880 | tf_op jit(solution)/shard_map/reduce_scatter | solution.py:249
  445.9 8.3 copy-start.110
  458.7 5.5 copy-start.22
  458.7 5.5 copy-start.26
  458.7 411.6 %reduce-scatter.13.cloned.1.call-start = ((), (), s32[]{:S(2)}) async-start(), calls=%async_computation.18 | async-start | bytes 5242880 | tf_op jit(solution)/shard_map/reduce_scatter | solution.py:159
  467.0 482.6 %reduce-scatter.11.cloned.1.call-start = ((), (), s32[]{:S(2)}) async-start(), calls=%async_computation.15 | async-start | bytes 5242880 | tf_op jit(solution)/shard_map/reduce_scatter | solution.py:159
  473.9 526.7 %reduce-scatter.23.cloned.1.call-start = ((), (), s32[]{:S(2)}) async-start(), calls=%async_computation.25 | async-start | bytes 3538944 | tf_op jit(solution)/shard_map/reduce_scatter | solution.py:260
  482.5 573.3 %reduce-scatter.27.cloned.1.call-start = ((), (), s32[]{:S(2)}) async-start(), calls=%async_computation.27 | async-start | bytes 4718592 | tf_op jit(solution)/shard_map/reduce_scatter | solution.py:262
  492.0 138.7 %copy-start.4 = (bf16[2,256,1024]{2,1,0:T(8,128)(2,1)S(1)}, bf16[2,256,1024]{2,1,0:T(8,128)(2,1)}, u32[]{:S(2)}) copy-start(bf16[2,256,1024]{2,1,0:T(8,128)(2,1)} %param.40) | copy-start | bytes 3145732
  492.0 138.7 %copy-start.83 = (f32[1024]{0:T(1024)S(1)}, f32[1024]{0:T(1024)}, u32[]{:S(2)}) copy-start(f32[1024]{0:T(1024)} %param.44) | copy-start | bytes 12292
  492.0 138.7 %copy-start.91 = (f32[256]{0:T(256)S(1)}, f32[256]{0:T(256)}, u32[]{:S(2)}) copy-start(f32[256]{0:T(256)} %copy-done.90) | copy-start | bytes 3076
  492.0 138.7 %copy-start.93 = (f32[256]{0:T(256)S(1)}, f32[256]{0:T(256)}, u32[]{:S(2)}) copy-start(f32[256]{0:T(256)} %copy-done.92) | copy-start | bytes 3076
  492.0 140.7 %copy-start.101 = (f32[256]{0:T(256)S(1)}, f32[256]{0:T(256)}, u32[]{:S(2)}) copy-start(f32[256]{0:T(256)} %copy-done.100) | copy-start | bytes 3076
  492.0 140.7 %copy-start.99 = (f32[256]{0:T(256)S(1)}, f32[256]{0:T(256)}, u32[]{:S(2)}) copy-start(f32[256]{0:T(256)} %copy-done.98) | copy-start | bytes 3076
  492.0 297.6 %copy-start.82 = (f32[1024]{0:T(1024)S(1)}, f32[1024]{0:T(1024)}, u32[]{:S(2)}) copy-start(f32[1024]{0:T(1024)} %param.46) | copy-start | bytes 12292
  492.0 297.6 %copy-start.95 = (f32[256]{0:T(256)S(1)}, f32[256]{0:T(256)}, u32[]{:S(2)}) copy-start(f32[256]{0:T(256)} %copy-done.94) | copy-start | bytes 3076
  492.0 297.6 %copy-start.97 = (f32[256]{0:T(256)S(1)}, f32[256]{0:T(256)}, u32[]{:S(2)}) copy-start(f32[256]{0:T(256)} %copy-done.96) | copy-start | bytes 3076
  710.2 82.8 %copy-start.14 = (f32[1,256,1024]{2,1,0:T(8,128)S(1)}, f32[1,256,1024]{2,1,0:T(8,128)}, u32[]{:S(2)}) copy-start(f32[1,256,1024]{2,1,0:T(8,128)} %reduce-scatter.21.cloned.1.call-done) | copy-start | bytes 3145732
  792.9 156.7 %copy-start.13 = (f32[1,256,1024]{2,1,0:T(8,128)S(1)}, f32[1,256,1024]{2,1,0:T(8,128)}, u32[]{:S(2)}) copy-start(f32[1,256,1024]{2,1,0:T(8,128)} %reduce-scatter.19.cloned.1.call-done) | copy-start | bytes 3145732
  792.9 156.7 %copy-start.102 = (f32[1024]{0:T(1024)S(1)}, f32[1024]{0:T(1024)}, u32[]{:S(2)}) copy-start(f32[1024]{0:T(1024)} %param.55) | copy-start | bytes 12292
  792.9 156.7 %copy-start.103 = (f32[1024]{0:T(1024)S(1)}, f32[1024]{0:T(1024)}, u32[]{:S(2)}) copy-start(f32[1024]{0:T(1024)} %param.51) | copy-start | bytes 12292
  839.7 216.1 %copy-start.104 = (f32[1024]{0:T(1024)}, f32[1024]{0:T(1024)S(1)}, u32[]{:S(2)}) copy-start(f32[1024]{0:T(1024)S(1)} %get-tuple-element.342) | copy-start | bytes 12292
  (87 other events, 239.8 us)
Sparse Core Ops, SparseCore 0:
  9.9 29.7 all-gather.11
  41.9 45.9 all-gather.9
  89.4 44.6 all-gather.19
  135.5 44.6 all-gather.23
  181.6 44.6 all-gather.25
  228.3 44.6 all-gather.21
  274.9 26.5 all-gather.15
  303.7 45.9 all-gather.13
  351.5 26.6 all-gather.17
  381.2 36.0 reduce-scatter.24
  420.7 51.3 reduce-scatter.28
  474.3 76.7 reduce-scatter.14
  553.4 77.2 reduce-scatter.18
  632.9 77.2 reduce-scatter.20
  712.3 77.2 reduce-scatter.16
  791.9 78.3 reduce-scatter.12
  872.4 77.2 reduce-scatter.10
  953.8 46.7 reduce-scatter.22
  1004.5 51.2 reduce-scatter.26
where the time goes:
time: 1070 us; the launch traced here: 1060 us
  waiting for transfers between devices  709 us (66%)
  matrix products  181 us (17%)
  blocking collectives  72.7 us (7%)
  other arithmetic  48.3 us (5%)
  local copies, waits for them, and re-layouts  35.3 us (3%)
  between operations  16.4 us (2%)
    reduce_scatter x2, waiting for transfers between devices, on_device(): lax.psum_scatter(grad_two, 'tensor', scatter_dimension=1, tiled=True)  157 us
    reduce_scatter x2, waiting for transfers between devices, on_device(): lax.psum_scatter(grad_one, 'tensor', scatter_dimension=1, tiled=True)  119 us
    reduce_scatter x2, waiting for transfers between devices, on_device(): lax.psum_scatter(partial_sum, 'tensor', scatter_dimension=1, tiled=True)  110 us
    all_gather x2, waiting for transfers between devices, on_device(): lax.all_gather(value_one.astype(jnp.bfloat16), 'tensor', axis=1, tiled=True)  85.3 us
    all_gather x2, waiting for transfers between devices, on_device(): lax.all_gather(value_two.astype(jnp.bfloat16), 'tensor', axis=1, tiled=True)  62.8 us
    reduce_scatter x1, waiting for transfers between devices, on_device(): lax.psum_scatter(grad_upw, 'dp', scatter_dimension=0, tiled=True)  55.3 us
    reduce_scatter x1, waiting for transfers between devices, on_device(): lax.psum_scatter(grad_qkv, 'dp', scatter_dimension=0, tiled=True)  45.7 us
    psum x1, blocking collectives, on_device(): lax.psum((sum_gain_one, sum_bias_one, sum_gain_two, sum_bias_two, sum_slo...  44 us
  transfers between devices with their start and end apart: 19, of which 16 were waited for; matrix products, arithmetic and copies ran while one was open for 23% of the time, Pallas kernels for 0%

commit v1 on v0

v1 whole, which is shorter than its diff:
```python
import jax
import jax.numpy as jnp
from jax import lax
from jax.sharding import PartitionSpec as P

HEAD = 64
ROT = 16
BLOCK = 256
F32 = jnp.float32
BF16 = jnp.bfloat16


def rope_tables(length):
    halved = ROT // 2
    frequency = 1.0 / 10000.0 ** (jnp.arange(halved, dtype=F32) * (2.0 / ROT))
    angles = jnp.arange(length, dtype=F32)[:, None] * frequency[None, :]
    angles = jnp.concatenate([angles, angles], axis=1)[:, None, :]
    return jnp.cos(angles), jnp.sin(angles)


def rotate(rows, cos_table, sin_table):
    halved = ROT // 2
    moving = rows[..., :ROT]
    turned = jnp.concatenate([-moving[..., halved:], moving[..., :halved]], axis=-1)
    moving = moving * cos_table + turned * sin_table
    return jnp.concatenate([moving, rows[..., ROT:]], axis=-1)


def visible(ids, limit, first, rows, key_end):
    own = ids[first : first + rows]
    pos = jnp.arange(key_end, dtype=jnp.int32)
    allowed = (ids[None, :key_end] <= own[:, None]) & (pos[None, :] < limit)
    return allowed[None]


def gelu_exact(v):
    return jax.nn.gelu(v, approximate=False)


def xor_pairs(n, mask):
    return [(i, i ^ mask) for i in range(n)]


def gather_line(block, axis, n):
    me = lax.axis_index(axis)
    right, left = block, block
    rights, lefts = [], []
    for s in range(1, n):
        right = lax.ppermute(right, axis, [(i, i + 1) for i in range(s - 1, n - 1)])
        left = lax.ppermute(left, axis, [(i, i - 1) for i in range(1, n - s + 1)])
        rights.append(right)
        lefts.append(left)
    line = jnp.concatenate(rights[::-1] + [block] + lefts, axis=0)
    rows = block.shape[0]
    return lax.dynamic_slice_in_dim(line, (n - 1 - me) * rows, n * rows, axis=0)


def scatter_line(partial, axis, n):
    me = lax.axis_index(axis)
    rows = partial.shape[0] // n

    def piece(index):
        index = jnp.clip(index, 0, n - 1)
        return lax.dynamic_slice_in_dim(partial, index * rows, rows, axis=0)

    from_left, from_right = None, None
    for s in range(1, n):
        to_right = piece(n - s + me)
        to_left = piece(s + me - n)
        if from_left is not None:
            to_right = to_right + from_left.astype(F32)
            to_left = to_left + from_right.astype(F32)
        from_left = lax.ppermute(to_right.astype(BF16), axis, [(i, i + 1) for i in range(0, s)])
        from_right = lax.ppermute(
            to_left.astype(BF16), axis, [(i, i - 1) for i in range(n - s, n)]
        )
    return piece(me) + from_left.astype(F32) + from_right.astype(F32)


def bits_of(n):
    return [1 << k for k in range(n.bit_length() - 1)]


def gather_cube(shard, axis, n, order):
    me = lax.axis_index(axis)
    pieces = {0: shard}
    for bit in order:
        new = {}
        held = sorted(pieces)
        moved = lax.ppermute(
            jnp.concatenate([pieces[m] for m in held], axis=0), axis, xor_pairs(n, bit)
        )
        rows = shard.shape[0]
        for k, m in enumerate(held):
            new[m] = pieces[m]
            new[m ^ bit] = moved[k * rows : (k + 1) * rows]
        pieces = new
    rows = shard.shape[0]
    full = jnp.zeros((n * rows,) + shard.shape[1:], shard.dtype)
    for m in range(n):
        full = lax.dynamic_update_slice_in_dim(full, pieces[m], (me ^ m) * rows, axis=0)
    return full


def scatter_cube(grad, axis, n, order):
    me = lax.axis_index(axis)
    nbits = n.bit_length() - 1
    rows = grad.shape[0] // n
    part = grad.reshape((2,) * nbits + (rows, grad.shape[1]))
    for bit in order:
        dim = nbits - bit.bit_length()
        mine = (me // bit) % 2
        keep = lax.dynamic_slice_in_dim(part, mine, 1, axis=dim)
        send = lax.dynamic_slice_in_dim(part, 1 - mine, 1, axis=dim)
        got = lax.ppermute(send.astype(BF16), axis, xor_pairs(n, bit))
        part = keep + got.astype(F32)
    return part.reshape(rows, grad.shape[1])


def all_sum(vec, axis, n):
    for bit in bits_of(n):
        vec = vec + lax.ppermute(vec, axis, xor_pairs(n, bit))
    return vec


def make(n_dp, n_tp):
    def on_device(
        inputs,
        cotangent,
        lengths,
        block_ids,
        ln1_gain,
        ln1_bias,
        ln2_gain,
        ln2_bias,
        w_qkv,
        b_qkv,
        w_out,
        b_out,
        w_up,
        b_up,
        w_down,
        b_down,
    ):
        seqs, own_rows, width = inputs.shape
        length = block_ids.shape[1]
        tile = min(512, length)
        heads = w_qkv.shape[1] // (3 * HEAD)
        scaling = HEAD ** (-0.5)
        cos_table, sin_table = rope_tables(length)
        starts = list(range(0, length, tile))
        ends = [min(length, first + tile + BLOCK) for first in starts]
        bits = bits_of(n_dp)
        asc = bits[1:] + bits[:1]
        desc = bits[1:][::-1] + bits[:1]

        x_all = [gather_line(inputs[i], "tensor", n_tp) for i in range(seqs)]
        qkv_w = gather_cube(w_qkv, "dp", n_dp, asc)
        up_w = gather_cube(w_up, "dp", n_dp, desc)
        down_w = gather_cube(w_down, "dp", n_dp, asc)
        out_w = gather_cube(w_out, "dp", n_dp, desc)
        c_all = [gather_line(cotangent[i], "tensor", n_tp) for i in range(seqs)]

        def dot(a, b, dims):
            return lax.dot_general(a, b, (dims, ((), ())), preferred_element_type=F32)

        def norm_stats(v):
            centre = jnp.mean(v, axis=-1, keepdims=True)
            shifted = v - centre
            spread = jnp.mean(shifted * shifted, axis=-1, keepdims=True)
            return centre, lax.rsqrt(spread + 1e-05)

        kept = []
        out_rows = []
        for i in range(seqs):
            res = x_all[i].astype(F32)
            centre, inv = norm_stats(res)
            xhat = (res - centre) * inv
            one = (xhat * ln1_gain + ln1_bias).astype(BF16)
            two = (xhat * ln2_gain + ln2_bias).astype(BF16)
            projected = (dot(one, qkv_w, ((1,), (0,))) + b_qkv).reshape(length, heads, 3, HEAD)
            queries = rotate(projected[:, :, 0], cos_table, sin_table).astype(BF16)
            keys = rotate(projected[:, :, 1], cos_table, sin_table).astype(BF16)
            values = projected[:, :, 2].astype(BF16)
            q_hd = (queries * BF16(scaling)).transpose(1, 0, 2)
            k_hd = keys.transpose(1, 0, 2)
            v_hd = values.transpose(1, 0, 2)
            logs, mixed = [], []
            for first, end in zip(starts, ends):
                allowed = visible(block_ids[i], lengths[i], first, tile, end)
                scores = jnp.einsum(
                    "hqe,hke->hqk",
                    q_hd[:, first : first + tile],
                    k_hd[:, :end],
                    preferred_element_type=F32,
                )
                scores = jnp.where(allowed, scores, -1e30)
                peak = jnp.max(scores, axis=-1)
                powered = jnp.exp(scores - peak[..., None])
                total = jnp.sum(powered, axis=-1)
                soft_low = (powered / total[..., None]).astype(BF16)
                logs.append(peak + jnp.log(total))
                mixed.append(
                    jnp.einsum("hqk,hke->hqe", soft_low, v_hd[:, :end], preferred_element_type=F32)
                )
            attended = (
                jnp.concatenate(mixed, axis=1)
                .transpose(1, 0, 2)
                .reshape(length, heads * HEAD)
                .astype(BF16)
            )
            hidden = dot(two, up_w, ((1,), (0,))) + b_up
            activated = gelu_exact(hidden).astype(BF16)
            partial = dot(attended, out_w, ((1,), (1,))) + dot(activated, down_w, ((1,), (1,)))
            reduced = scatter_line(partial, "tensor", n_tp)
            out_rows.append((inputs[i].astype(F32) + reduced + b_out + b_down).astype(BF16))
            kept.append((one, two, q_hd, k_hd, v_hd, logs, attended, hidden, activated))

        g_qkv = g_out = g_up = g_down = None
        s_qkv = s_up = s_g1 = s_b1 = s_g2 = s_b2 = s_slope = 0.0
        grad_rows = []

        def add(total, new):
            return new if total is None else total + new

        for i in range(seqs):
            one, two, q_hd, k_hd, v_hd, logs, attended, hidden, activated = kept[i]
            slope = c_all[i]
            g_out = add(g_out, dot(slope, attended, ((0,), (0,))))
            g_down = add(g_down, dot(slope, activated, ((0,), (0,))))
            grad_att = dot(slope, out_w, ((1,), (0,))).astype(BF16)
            grad_att = grad_att.reshape(length, heads, HEAD).transpose(1, 0, 2)
            grad_act = dot(slope, down_w, ((1,), (0,)))
            cdf = 0.5 * (1.0 + lax.erf(hidden * (0.5**0.5)))
            pdf = jnp.exp(-0.5 * hidden * hidden) * 0.3989422804014327
            grad_hidden = (grad_act * (cdf + hidden * pdf)).astype(BF16)
            g_up = add(g_up, dot(two, grad_hidden, ((0,), (0,))))
            s_up = s_up + jnp.sum(grad_hidden.astype(F32), axis=0)
            grad_two = dot(grad_hidden, up_w, ((1,), (1,)))
            gk = jnp.zeros((heads, length, HEAD), F32)
            gv = jnp.zeros((heads, length, HEAD), F32)
            gq = []
            for n, first in enumerate(starts):
                end = ends[n]
                q_t = q_hd[:, first : first + tile]
                g_t = grad_att[:, first : first + tile]
                k_t = k_hd[:, :end]
                allowed = visible(block_ids[i], lengths[i], first, tile, end)
                scores = jnp.einsum("hqe,hke->hqk", q_t, k_t, preferred_element_type=F32)
                scores = jnp.where(allowed, scores, -1e30)
                soft = jnp.exp(scores - logs[n][..., None])
                gv = gv.at[:, :end].add(
                    jnp.einsum("hqk,hqe->hke", soft.astype(BF16), g_t, preferred_element_type=F32)
                )
                grad_soft = jnp.einsum(
                    "hqe,hke->hqk", g_t, v_hd[:, :end], preferred_element_type=F32
                )
                centred = jnp.sum(soft * grad_soft, axis=-1)
                gs = (soft * (grad_soft - centred[..., None])).astype(BF16)
                gq.append(
                    jnp.einsum("hqk,hke->hqe", gs, k_t, preferred_element_type=F32) * scaling
                )
                gk = gk.at[:, :end].add(
                    jnp.einsum("hqk,hqe->hke", gs, q_t, preferred_element_type=F32)
                )
            gq = jnp.concatenate(gq, axis=1).transpose(1, 0, 2)
            gk = gk.transpose(1, 0, 2)
            gv = gv.transpose(1, 0, 2)
            gp = jnp.stack(
                [rotate(gq, cos_table, -sin_table), rotate(gk, cos_table, -sin_table), gv], axis=2
            )
            gp = gp.reshape(length, 3 * heads * HEAD).astype(BF16)
            g_qkv = add(g_qkv, dot(one, gp, ((0,), (0,))))
            s_qkv = s_qkv + jnp.sum(gp.astype(F32), axis=0)
            grad_one = dot(gp, qkv_w, ((1,), (1,)))
            res = x_all[i].astype(F32)
            centre, inv = norm_stats(res)
            xhat = (res - centre) * inv
            s_g1 = s_g1 + jnp.sum(grad_one * xhat, axis=0)
            s_b1 = s_b1 + jnp.sum(grad_one, axis=0)
            s_g2 = s_g2 + jnp.sum(grad_two * xhat, axis=0)
            s_b2 = s_b2 + jnp.sum(grad_two, axis=0)
            both = grad_one * ln1_gain + grad_two * ln2_gain
            e = scatter_line(both, "tensor", n_tp)
            mine = inputs[i].astype(F32)
            centre, inv = norm_stats(mine)
            xh = (mine - centre) * inv
            slope_own = cotangent[i].astype(F32)
            back = (
                e
                - jnp.mean(e, axis=-1, keepdims=True)
                - xh * jnp.mean(e * xh, axis=-1, keepdims=True)
            ) * inv
            grad_rows.append(slope_own + back)
            s_slope = s_slope + jnp.sum(slope_own, axis=0)
        r_asc = bits[:1] + bits[1:]
        r_desc = bits[:1] + bits[1:][::-1]
        o_down = scatter_cube(g_down, "dp", n_dp, r_asc)
        o_out = scatter_cube(g_out, "dp", n_dp, r_desc)
        o_up = scatter_cube(g_up, "dp", n_dp, r_desc)
        o_qkv = scatter_cube(g_qkv, "dp", n_dp, r_asc)
        vec = jnp.concatenate([s_g1, s_b1, s_g2, s_b2, s_slope, s_qkv, s_up])
        vec = all_sum(vec, "dp", n_dp)
        shared = all_sum(vec[: 5 * width], "tensor", n_tp).reshape(5, width)
        q_cols = w_qkv.shape[1]
        return (
            jnp.stack(out_rows),
            jnp.stack(grad_rows),
            o_qkv,
            o_out,
            o_up,
            o_down,
            vec[5 * width : 5 * width + q_cols],
            vec[5 * width + q_cols :],
            shared[0],
            shared[1],
            shared[2],
            shared[3],
            shared[4],
            shared[4],
        )

    return on_device


def solution(mesh):
    in_specs = (
        P("dp", "tensor", None),
        P("dp", "tensor", None),
        P("dp"),
        P("dp", None),
        P(),
        P(),
        P(),
        P(),
        P("dp", "tensor"),
        P("tensor"),
        P("dp", "tensor"),
        P(),
        P("dp", "tensor"),
        P("tensor"),
        P("dp", "tensor"),
        P(),
    )
    out_specs = (
        P("dp", "tensor", None),
        P("dp", "tensor", None),
        P("dp", "tensor"),
        P("dp", "tensor"),
        P("dp", "tensor"),
        P("dp", "tensor"),
        P("tensor"),
        P("tensor"),
        P(),
        P(),
        P(),
        P(),
        P(),
        P(),
    )
    return jax.shard_map(
        make(mesh.shape["dp"], mesh.shape["tensor"]),
        mesh=mesh,
        in_specs=in_specs,
        out_specs=out_specs,
        check_vma=False,
    )
```

time: 1070 us -> 613 us (0.57)
  waiting for transfers between devices: 709 us -> 195 us
  starting transfers between devices: 1.4 us -> 157 us
  blocking collectives: 72.7 us -> 0 us
  matrix products: 181 us -> 142 us
  between operations: 16.4 us -> 4.26 us
  local copies, waits for them, and re-layouts: 35.3 us -> 46.3 us
    reduce_scatter x10 -> x0, waiting for transfers between devices: 487 us -> none  [the longest x2 157 us: on_device(): lax.psum_scatter(grad_two, 'tensor', scatter_dimension=1, tiled=True)]
    all_gather x9 -> x0, waiting for transfers between devices: 218 us -> none  [the longest x2 85.3 us: on_device(): lax.all_gather(value_one.astype(jnp.bfloat16), 'tensor', axis=1, tiled=True)]
    ppermute x0 -> x77, waiting for transfers between devices: none -> 195 us  [the longest x12 94 us: gather_line(): left = lax.ppermute(left, axis, [(i, i - 1) for i in range(1, n - s + 1)])]
    ppermute x0 -> x77, starting transfers between devices: none -> 157 us  [the longest x12 64.2 us: scatter_line(): lax.ppermute(to_right.astype(BF16), axis, [(i, i + 1) for i in range(0, s)])]
    psum x2 -> x0, blocking collectives: 59.9 us -> none  [the longest x1 44 us: on_device(): lax.psum((sum_gain_one, sum_bias_one, sum_gain_two, sum_bias_two, sum_slo...]
    dot_general x48, matrix products: 181 us -> 142 us  [the longest x24 89.3 us: dot(): return lax.dot_general(a, b, (dims, ((), ())), preferred_element_type=F32)]
    dynamic_update_slice x0 -> x31, local copies, waits for them, and re-layouts: none -> 12.9 us  [gather_cube(): lax.dynamic_update_slice_in_dim(full, pieces[m], (me ^ m) * rows, axis=0)]
    all_gather x1 -> x0, blocking collectives: 12.7 us -> none  [on_device(): lax.all_gather(w_out, 'dp', axis=0, tiled=True)]
  transfers between devices with their start and end apart: 19 -> 77, of which waited for: 16 -> 29; matrix products, arithmetic and copies ran while one was open for 23% -> 39% of each run, Pallas kernels for 0% -> 0%
where the time goes in v1:
time: 613 us; the launch traced here: 603 us
  waiting for transfers between devices  195 us (32%)
  starting transfers between devices  157 us (26%)
  matrix products  142 us (23%)
  other arithmetic  58.3 us (10%)
  local copies, waits for them, and re-layouts  46.3 us (8%)
    ppermute x12, waiting for transfers between devices, gather_line(): left = lax.ppermute(left, axis, [(i, i - 1) for i in range(1, n - s + 1)])  94 us
    dot_general x24, matrix products, dot(): return lax.dot_general(a, b, (dims, ((), ())), preferred_element_type=F32)  89.3 us
    ppermute x12, starting transfers between devices, scatter_line(): lax.ppermute(to_right.astype(BF16), axis, [(i, i + 1) for i in range(0, s)])  64.2 us
    ppermute x12, waiting for transfers between devices, scatter_line(): lax.ppermute(to_right.astype(BF16), axis, [(i, i + 1) for i in range(0, s)])  59.2 us
    ppermute x12, starting transfers between devices, gather_line(): right = lax.ppermute(right, axis, [(i, i + 1) for i in range(s - 1, n - 1)])  21.8 us
    ppermute x12, starting transfers between devices, scatter_cube(): got = lax.ppermute(send.astype(BF16), axis, xor_pairs(n, bit))  18.6 us
    ppermute x12, waiting for transfers between devices, scatter_line(): lax.ppermute(to_left.astype(BF16), axis, [(i, i - 1) for i in range(n - s...  16.8 us
    ppermute x12, starting transfers between devices, gather_line(): left = lax.ppermute(left, axis, [(i, i - 1) for i in range(1, n - s + 1)])  15.4 us
  transfers between devices with their start and end apart: 77, of which 29 were waited for; matrix products, arithmetic and copies ran while one was open for 39% of the time, Pallas kernels for 0%

profile of v1, /device:TPU:0, one launch (start us, length us, event | category | flops | bytes accessed | tf_op | source)
XLA Modules:
  0.0 602.5 jit_solution(14076415395282316063)
XLA Ops:
  0.7 3.0 collective-permute-start.9
  5.7 4.7 collective-permute-start.15
  12.6 4.6 collective-permute-start
  34.5 2.5 collective-permute-done.10
  37.1 2.6 collective-permute-start.24
  48.4 5.4 collective-permute-done.7
  57.1 7.4 %collective-permute-done.16 = bf16[256,1024]{1,0:T(8,128)(2,1)S(1)} collective-permute-done((bf16[256,1024]{1,0:T(8,128)(2,1)S(1)}, bf16[256,1024]{1,0:T(8,128)(2,1)S(1)}, u32[]{:S(2)}, u32[]{:S(2)}) %collective-permute-start.16) | collective-permute-done | bytes 524320 | tf_op jit(solution)/shard_map/ppermute | solution.py:90
  64.6 3.4 collective-permute-start.48
  77.3 19.0 %collective-permute-done.3 = bf16[256,1024]{1,0:T(8,128)(2,1)S(1)} collective-permute-done((bf16[256,1024]{1,0:T(8,128)(2,1)}, bf16[256,1024]{1,0:T(8,128)(2,1)S(1)}, u32[]{:S(2)}, u32[]{:S(2)}) %collective-permute-start.3) | collective-permute-done | bytes 524320 | tf_op jit(solution)/shard_map/ppermute | solution.py:50
  99.1 5.2 collective-permute-start.36
  105.8 7.4 %collective-permute-done.27 = bf16[256,1024]{1,0:T(8,128)(2,1)S(1)} collective-permute-done((bf16[256,1024]{1,0:T(8,128)(2,1)S(1)}, bf16[256,1024]{1,0:T(8,128)(2,1)S(1)}, u32[]{:S(2)}, u32[]{:S(2)}) %collective-permute-start.27) | collective-permute-done | bytes 524320 | tf_op jit(solution)/shard_map/ppermute | solution.py:50
  114.4 7.4 %collective-permute-done.4 = bf16[256,1024]{1,0:T(8,128)(2,1)S(1)} collective-permute-done((bf16[256,1024]{1,0:T(8,128)(2,1)S(1)}, bf16[256,1024]{1,0:T(8,128)(2,1)S(1)}, u32[]{:S(2)}, u32[]{:S(2)}) %collective-permute-start.4) | collective-permute-done | bytes 524320 | tf_op jit(solution)/shard_map/ppermute | solution.py:50
  126.4 8.1 %collective-permute-done.39 = bf16[256,1024]{1,0:T(8,128)(2,1)S(1)} collective-permute-done((bf16[256,1024]{1,0:T(8,128)(2,1)S(1)}, bf16[256,1024]{1,0:T(8,128)(2,1)S(1)}, u32[]{:S(2)}, u32[]{:S(2)}) %collective-permute-start.39) | collective-permute-done | bytes 524320 | tf_op jit(solution)/shard_map/ppermute | solution.py:50
  135.2 10.5 %collective-permute-done.28 = bf16[256,1024]{1,0:T(8,128)(2,1)S(1)} collective-permute-done((bf16[256,1024]{1,0:T(8,128)(2,1)S(1)}, bf16[256,1024]{1,0:T(8,128)(2,1)S(1)}, u32[]{:S(2)}, u32[]{:S(2)}) %collective-permute-start.28) | collective-permute-done | bytes 524320 | tf_op jit(solution)/shard_map/ppermute | solution.py:50
  147.0 9.9 %collective-permute-done.5 = bf16[256,1024]{1,0:T(8,128)(2,1)S(1)} collective-permute-done((bf16[256,1024]{1,0:T(8,128)(2,1)S(1)}, bf16[256,1024]{1,0:T(8,128)(2,1)S(1)}, u32[]{:S(2)}, u32[]{:S(2)}) %collective-permute-start.5) | collective-permute-done | bytes 524320 | tf_op jit(solution)/shard_map/ppermute | solution.py:50
  162.3 27.3 %collective-permute-done.29 = bf16[256,1024]{1,0:T(8,128)(2,1)S(1)} collective-permute-done((bf16[256,1024]{1,0:T(8,128)(2,1)S(1)}, bf16[256,1024]{1,0:T(8,128)(2,1)S(1)}, u32[]{:S(2)}, u32[]{:S(2)}) %collective-permute-start.29) | collective-permute-done | bytes 524320 | tf_op jit(solution)/shard_map/ppermute | solution.py:50
  204.4 2.8 fusion.128
  208.9 4.3 collective-permute-done.53
  216.4 2.6 multiply_reduce_fusion.2
  224.4 2.6 fusion.78
  230.9 2.9 fusion.129
  233.8 2.6 fusion.80
  236.4 2.6 multiply_reduce_fusion.3
  244.8 2.5 fusion
  247.3 3.3 fusion.127
  250.6 3.0 multiply_reduce_fusion.1
  262.4 2.7 fusion.1
  265.1 3.3 fusion.126
  268.4 4.2 multiply_reduce_fusion
  272.6 3.5 multiply_convert_fusion
  276.1 3.8 convolution_multiply_fusion
  290.8 2.7 collective-permute-start.63
  304.2 5.7 collective-permute-start.60
  309.9 3.9 fusion.253
  313.8 3.9 fusion.254
  327.3 22.2 %fusion.38 = (bf16[1024,1024]{1,0:T(8,128)(2,1)}, bf16[1024,1024]{1,0:T(8,128)(2,1)S(1)}, f32[1024,1024]{1,0:T(8,128)}) fusion(f32[1024]{0:T(1024)S(1)} %copy-done.94, f32[1024,1024]{1,0:T(8,128)S(1)} %fusion.228, bf16[1024,1024]{1,0:T(8,128)(2,1)S(1)} %slice_dynamic-update-slice_fusion.6, f32[1024]{0:T(1024)S(1)} %copy-done.95, f32[1024]{0:T(1024)S(1)} %copy-done.96, ...), kind=kOutput, calls=%fused_computation.68 | convolution fusion | flops 2292187136 | bytes 16797700 | tf_op jit(solution)/shard_map/dot_general | solution.py:165
  353.5 4.9 convert_reduce_fusion.2
  363.4 2.7 fusion.226
  366.7 5.2 convert_reduce_fusion.3
  371.8 4.6 convolution_add_fusion.3
  379.9 4.2 convolution_add_fusion.2
  387.8 4.3 collective-permute-start.18
  394.0 6.3 %fusion.234 = (f32[1024]{0:T(1024)S(1)}, f32[1024]{0:T(1024)S(1)}, f32[1024,1024]{1,0:T(8,128)S(1)}, f32[1024]{0:T(1024)S(1)}, f32[1024]{0:T(1024)S(1)}) fusion(f32[1024]{0:T(1024)S(1)} %copy-done.91, f32[1024]{0:T(1024)S(1)} %copy-done.84, bf16[1792,1024]{1,0:T(8,128)(2,1)S(1)} %copy-done.8, s32[]{:T(128)S(6)} %select_n.200, f32[1024]{0:T(1024)S(1)} %copy-done.96, ...), kind=kOutput, calls=%fused_computation.497 | convolution fusion | flops 2160062464 | bytes 14712836 | tf_op jit(solution)/shard_map/dot_general | solution.py:165
  400.3 6.3 %fusion.233 = (f32[1024]{0:T(1024)S(1)}, f32[1024]{0:T(1024)S(1)}, f32[1024,1024]{1,0:T(8,128)S(1)}, f32[1024]{0:T(1024)S(1)}, f32[1024]{0:T(1024)S(1)}) fusion(f32[1024]{0:T(1024)S(1)} %add_rsqrt_fusion, f32[1024]{0:T(1024)S(1)} %broadcast_multiply_fusion, bf16[1792,1024]{1,0:T(8,128)(2,1)S(1)} %copy-done.6, s32[]{:T(128)S(6)} %select_n.200, ...), kind=kOutput, calls=%fused_computation.496 | convolution fusion | flops 2160062464 | bytes 14712836 | tf_op jit(solution)/shard_map/dot_general | solution.py:165
  408.5 2.6 collective-permute-done.65
  418.6 6.2 %collective-permute-done.30 = bf16[256,1024]{1,0:T(8,128)(2,1)S(1)} collective-permute-done((bf16[256,1024]{1,0:T(8,128)(2,1)S(1)}, bf16[256,1024]{1,0:T(8,128)(2,1)S(1)}, u32[]{:S(2)}, u32[]{:S(2)}) %collective-permute-start.30) | collective-permute-done | bytes 524320 | tf_op jit(solution)/shard_map/ppermute | solution.py:73
  425.7 10.4 %collective-permute-done.54 = bf16[256,1024]{1,0:T(8,128)(2,1)S(1)} collective-permute-done((bf16[256,1024]{1,0:T(8,128)(2,1)S(1)}, bf16[256,1024]{1,0:T(8,128)(2,1)S(1)}, u32[]{:S(2)}, u32[]{:S(2)}) %collective-permute-start.54) | collective-permute-done | bytes 524320 | tf_op jit(solution)/shard_map/ppermute | solution.py:73
  437.7 7.4 %collective-permute-done.42 = bf16[256,1024]{1,0:T(8,128)(2,1)S(1)} collective-permute-done((bf16[256,1024]{1,0:T(8,128)(2,1)S(1)}, bf16[256,1024]{1,0:T(8,128)(2,1)S(1)}, u32[]{:S(2)}, u32[]{:S(2)}) %collective-permute-start.42) | collective-permute-done | bytes 524320 | tf_op jit(solution)/shard_map/ppermute | solution.py:73
  446.8 4.4 collective-permute-start.19
  457.2 6.3 %collective-permute-done.19 = bf16[256,1024]{1,0:T(8,128)(2,1)S(1)} collective-permute-done((bf16[256,1024]{1,0:T(8,128)(2,1)S(1)}, bf16[256,1024]{1,0:T(8,128)(2,1)S(1)}, u32[]{:S(2)}, u32[]{:S(2)}) %collective-permute-start.19) | collective-permute-done | bytes 524320 | tf_op jit(solution)/shard_map/ppermute | solution.py:73
  463.6 4.4 collective-permute-start.55
  470.3 4.5 collective-permute-done.31
  477.3 8.7 %collective-permute-done.55 = bf16[256,1024]{1,0:T(8,128)(2,1)S(1)} collective-permute-done((bf16[256,1024]{1,0:T(8,128)(2,1)S(1)}, bf16[256,1024]{1,0:T(8,128)(2,1)S(1)}, u32[]{:S(2)}, u32[]{:S(2)}) %collective-permute-start.55) | collective-permute-done | bytes 524320 | tf_op jit(solution)/shard_map/ppermute | solution.py:73
  486.1 4.4 collective-permute-start.20
  491.6 5.7 collective-permute-done.43
  500.4 29.7 %collective-permute-start.44 = (bf16[256,1024]{1,0:T(8,128)(2,1)S(1)}, bf16[256,1024]{1,0:T(8,128)(2,1)S(1)}, u32[]{:S(2)}, u32[]{:S(2)}) collective-permute-start(bf16[256,1024]{1,0:T(8,128)(2,1)S(1)} %get-tuple-element.177), channel_id=1, source_target_pairs={{0,1},{1,2},{2,3},{4,5},{5,6},{6,7},{8,9},{9,10},{10,11},{12,13},{... | collective-permute-start | bytes 1572872 | tf_op jit(solution)/shard_map/ppermute | solution.py:73
  532.0 4.6 collective-permute-start.32
  536.8 4.5 collective-permute-start.56
  546.5 4.8 collective-permute-done.32
  551.8 5.0 collective-permute-done.56
  558.9 10.5 %collective-permute-done.35 = bf16[256,1024]{1,0:T(8,128)(2,1)S(1)} collective-permute-done((bf16[256,1024]{1,0:T(8,128)(2,1)S(1)}, bf16[256,1024]{1,0:T(8,128)(2,1)S(1)}, u32[]{:S(2)}, u32[]{:S(2)}) %collective-permute-start.35) | collective-permute-done | bytes 524320 | tf_op jit(solution)/shard_map/ppermute | solution.py:74
  569.4 5.7 collective-permute-done.59
  586.2 5.5 collective-permute-start.75
  593.5 3.0 collective-permute-start.76
  (561 shorter events, 207.7 us)
Async XLA Ops:
  0.7 30.1 %collective-permute-start.9 = (bf16[128,256]{1,0:T(8,128)(2,1)}, bf16[128,256]{1,0:T(8,128)(2,1)S(1)}, u32[]{:S(2)}, u32[]{:S(2)}) collective-permute-start(bf16[128,256]{1,0:T(8,128)(2,1)} %param.50), channel_id=1, source_target_pairs={{0,16},{4,20},{8,24},{12,28},{16,0},{20,4},{24,8},{28,12},{1,17},{... | collective-permute-start | bytes 196616 | tf_op jit(solution)/shard_map/ppermute | solution.py:90
  3.7 36.9 %collective-permute-start.6 = (bf16[128,768]{1,0:T(8,128)(2,1)}, bf16[128,768]{1,0:T(8,128)(2,1)}, u32[]{:S(2)}, u32[]{:S(2)}) collective-permute-start(bf16[128,768]{1,0:T(8,128)(2,1)} %param.48), channel_id=1, source_target_pairs={{0,8},{4,12},{8,0},{12,4},{16,24},{20,28},{24,16},{28,20},{1,9},{5... | collective-permute-start | bytes 589832 | tf_op jit(solution)/shard_map/ppermute | solution.py:90
  5.2 36.5 %collective-permute-start.12 = (bf16[128,1024]{1,0:T(8,128)(2,1)}, bf16[128,1024]{1,0:T(8,128)(2,1)}, u32[]{:S(2)}, u32[]{:S(2)}) collective-permute-start(bf16[128,1024]{1,0:T(8,128)(2,1)} %param.52), channel_id=1, source_target_pairs={{0,16},{4,20},{8,24},{12,28},{16,0},{20,4},{24,8},{28,12},{1,17},{... | collective-permute-start | bytes 786440 | tf_op jit(solution)/shard_map/ppermute | solution.py:90
  5.7 38.6 %collective-permute-start.15 = (bf16[128,1024]{1,0:T(8,128)(2,1)}, bf16[128,1024]{1,0:T(8,128)(2,1)}, u32[]{:S(2)}, u32[]{:S(2)}) collective-permute-start(bf16[128,1024]{1,0:T(8,128)(2,1)} %param.54), channel_id=1, source_target_pairs={{0,8},{4,12},{8,0},{12,4},{16,24},{20,28},{24,16},{28,20},{1,9},{5... | collective-permute-start | bytes 786440 | tf_op jit(solution)/shard_map/ppermute | solution.py:90
  12.6 43.1 %collective-permute-start = (bf16[256,1024]{1,0:T(8,128)(2,1)}, bf16[256,1024]{1,0:T(8,128)(2,1)}, u32[]{:S(2)}, u32[]{:S(2)}) collective-permute-start(bf16[256,1024]{1,0:T(8,128)(2,1)} %get-tuple-element.219), channel_id=1, source_target_pairs={{0,1},{1,2},{2,3},{4,5},{5,6},{6,7},{8,9},{9,10},{10,11},{12,13},{... | collective-permute-start | bytes 1572872 | tf_op jit(solution)/shard_map/ppermute | solution.py:49
  37.1 19.3 %collective-permute-start.24 = (bf16[256,1024]{1,0:T(8,128)(2,1)}, bf16[256,1024]{1,0:T(8,128)(2,1)S(1)}, u32[]{:S(2)}, u32[]{:S(2)}) collective-permute-start(bf16[256,1024]{1,0:T(8,128)(2,1)} %get-tuple-element.220), channel_id=1, source_target_pairs={{0,1},{1,2},{2,3},{4,5},{5,6},{6,7},{8,9},{9,10},{10,11},{12,13},{... | collective-permute-start | bytes 1572872 | tf_op jit(solution)/shard_map/ppermute | solution.py:49
  44.3 25.7 %collective-permute-start.13 = (bf16[256,1024]{1,0:T(8,128)(2,1)S(1)}, bf16[256,1024]{1,0:T(8,128)(2,1)S(1)}, u32[]{:S(2)}, u32[]{:S(2)}) collective-permute-start(bf16[256,1024]{1,0:T(8,128)(2,1)S(1)} %pad_maximum_fusion.6), channel_id=1, source_target_pairs={{0,8},{4,12},{8,0},{12,4},{16,24},{20,28},{24,16},{28,20},{1,9},{5... | collective-permute-start | bytes 1572872 | tf_op jit(solution)/shard_map/ppermute | solution.py:90
  46.8 17.7 %collective-permute-start.16 = (bf16[256,1024]{1,0:T(8,128)(2,1)S(1)}, bf16[256,1024]{1,0:T(8,128)(2,1)S(1)}, u32[]{:S(2)}, u32[]{:S(2)}) collective-permute-start(bf16[256,1024]{1,0:T(8,128)(2,1)S(1)} %pad_maximum_fusion.7), channel_id=1, source_target_pairs={{0,16},{4,20},{8,24},{12,28},{16,0},{20,4},{24,8},{28,12},{1,17},{... | collective-permute-start | bytes 1572872 | tf_op jit(solution)/shard_map/ppermute | solution.py:90
  54.7 20.8 %collective-permute-start.8 = (bf16[512,768]{1,0:T(8,128)(2,1)S(1)}, bf16[512,768]{1,0:T(8,128)(2,1)S(1)}, u32[]{:S(2)}, u32[]{:S(2)}) collective-permute-start(bf16[512,768]{1,0:T(8,128)(2,1)S(1)} %pad_maximum_fusion.4), channel_id=1, source_target_pairs={{0,4},{4,0},{8,12},{12,8},{16,20},{20,16},{24,28},{28,24},{1,5},{5... | collective-permute-start | bytes 2359304 | tf_op jit(solution)/shard_map/ppermute | solution.py:90
  55.7 17.8 %collective-permute-start.1 = (bf16[256,1024]{1,0:T(8,128)(2,1)}, bf16[256,1024]{1,0:T(8,128)(2,1)S(1)}, u32[]{:S(2)}, u32[]{:S(2)}) collective-permute-start(bf16[256,1024]{1,0:T(8,128)(2,1)} %collective-permute-done), channel_id=1, source_target_pairs={{1,2},{2,3},{5,6},{6,7},{9,10},{10,11},{13,14},{14,15},{17,18},{18... | collective-permute-start | bytes 1572872 | tf_op jit(solution)/shard_map/ppermute | solution.py:49
  56.4 18.4 %collective-permute-start.25 = (bf16[256,1024]{1,0:T(8,128)(2,1)S(1)}, bf16[256,1024]{1,0:T(8,128)(2,1)S(1)}, u32[]{:S(2)}, u32[]{:S(2)}) collective-permute-start(bf16[256,1024]{1,0:T(8,128)(2,1)S(1)} %collective-permute-done.24), channel_id=1, source_target_pairs={{1,2},{2,3},{5,6},{6,7},{9,10},{10,11},{13,14},{14,15},{17,18},{18... | collective-permute-start | bytes 1572872 | tf_op jit(solution)/shard_map/ppermute | solution.py:49
  64.6 39.9 %collective-permute-start.48 = (bf16[256,1024]{1,0:T(8,128)(2,1)S(1)}, bf16[256,1024]{1,0:T(8,128)(2,1)S(1)}, u32[]{:S(2)}, u32[]{:S(2)}) collective-permute-start(bf16[256,1024]{1,0:T(8,128)(2,1)S(1)} %copy-done.58), channel_id=1, source_target_pairs={{0,1},{1,2},{2,3},{4,5},{5,6},{6,7},{8,9},{9,10},{10,11},{12,13},{... | collective-permute-start | bytes 1572872 | tf_op jit(solution)/shard_map/ppermute | solution.py:49
  70.0 54.4 %collective-permute-start.51 = (bf16[256,1024]{1,0:T(8,128)(2,1)S(1)}, bf16[256,1024]{1,0:T(8,128)(2,1)S(1)}, u32[]{:S(2)}, u32[]{:S(2)}) collective-permute-start(bf16[256,1024]{1,0:T(8,128)(2,1)S(1)} %copy-done.58), channel_id=1, source_target_pairs={{1,0},{2,1},{3,2},{5,4},{6,5},{7,6},{9,8},{10,9},{11,10},{13,12},{... | collective-permute-start | bytes 1572872 | tf_op jit(solution)/shard_map/ppermute | solution.py:50
  73.5 22.9 %collective-permute-start.3 = (bf16[256,1024]{1,0:T(8,128)(2,1)}, bf16[256,1024]{1,0:T(8,128)(2,1)S(1)}, u32[]{:S(2)}, u32[]{:S(2)}) collective-permute-start(bf16[256,1024]{1,0:T(8,128)(2,1)} %get-tuple-element.219), channel_id=1, source_target_pairs={{1,0},{2,1},{3,2},{5,4},{6,5},{7,6},{9,8},{10,9},{11,10},{13,12},{... | collective-permute-start | bytes 1572872 | tf_op jit(solution)/shard_map/ppermute | solution.py:50
  74.8 24.3 %collective-permute-start.2 = (bf16[256,1024]{1,0:T(8,128)(2,1)S(1)}, bf16[256,1024]{1,0:T(8,128)(2,1)S(1)}, u32[]{:S(2)}, u32[]{:S(2)}) collective-permute-start(bf16[256,1024]{1,0:T(8,128)(2,1)S(1)} %collective-permute-done.1), channel_id=1, source_target_pairs={{2,3},{6,7},{10,11},{14,15},{18,19},{22,23},{26,27},{30,31}} | collective-permute-start | bytes 1572872 | tf_op jit(solution)/shard_map/ppermute | solution.py:49
  75.5 22.2 %collective-permute-start.26 = (bf16[256,1024]{1,0:T(8,128)(2,1)S(1)}, bf16[256,1024]{1,0:T(8,128)(2,1)S(1)}, u32[]{:S(2)}, u32[]{:S(2)}) collective-permute-start(bf16[256,1024]{1,0:T(8,128)(2,1)S(1)} %collective-permute-done.25), channel_id=1, source_target_pairs={{2,3},{6,7},{10,11},{14,15},{18,19},{22,23},{26,27},{30,31}} | collective-permute-start | bytes 1572872 | tf_op jit(solution)/shard_map/ppermute | solution.py:49
  96.4 16.7 %collective-permute-start.27 = (bf16[256,1024]{1,0:T(8,128)(2,1)S(1)}, bf16[256,1024]{1,0:T(8,128)(2,1)S(1)}, u32[]{:S(2)}, u32[]{:S(2)}) collective-permute-start(bf16[256,1024]{1,0:T(8,128)(2,1)S(1)} %copy-done.56), channel_id=1, source_target_pairs={{1,0},{2,1},{3,2},{5,4},{6,5},{7,6},{9,8},{10,9},{11,10},{13,12},{... | collective-permute-start | bytes 1572872 | tf_op jit(solution)/shard_map/ppermute | solution.py:50
  97.7 24.2 %collective-permute-start.4 = (bf16[256,1024]{1,0:T(8,128)(2,1)S(1)}, bf16[256,1024]{1,0:T(8,128)(2,1)S(1)}, u32[]{:S(2)}, u32[]{:S(2)}) collective-permute-start(bf16[256,1024]{1,0:T(8,128)(2,1)S(1)} %collective-permute-done.3), channel_id=1, source_target_pairs={{1,0},{2,1},{5,4},{6,5},{9,8},{10,9},{13,12},{14,13},{17,16},{18,1... | collective-permute-start | bytes 1572872 | tf_op jit(solution)/shard_map/ppermute | solution.py:50
  99.1 26.0 %collective-permute-start.36 = (bf16[256,1024]{1,0:T(8,128)(2,1)S(1)}, bf16[256,1024]{1,0:T(8,128)(2,1)S(1)}, u32[]{:S(2)}, u32[]{:S(2)}) collective-permute-start(bf16[256,1024]{1,0:T(8,128)(2,1)S(1)} %copy-done.57), channel_id=1, source_target_pairs={{0,1},{1,2},{2,3},{4,5},{5,6},{6,7},{8,9},{9,10},{10,11},{12,13},{... | collective-permute-start | bytes 1572872 | tf_op jit(solution)/shard_map/ppermute | solution.py:49
  104.5 30.0 %collective-permute-start.39 = (bf16[256,1024]{1,0:T(8,128)(2,1)S(1)}, bf16[256,1024]{1,0:T(8,128)(2,1)S(1)}, u32[]{:S(2)}, u32[]{:S(2)}) collective-permute-start(bf16[256,1024]{1,0:T(8,128)(2,1)S(1)} %copy-done.57), channel_id=1, source_target_pairs={{1,0},{2,1},{3,2},{5,4},{6,5},{7,6},{9,8},{10,9},{11,10},{13,12},{... | collective-permute-start | bytes 1572872 | tf_op jit(solution)/shard_map/ppermute | solution.py:50
  113.1 32.6 %collective-permute-start.28 = (bf16[256,1024]{1,0:T(8,128)(2,1)S(1)}, bf16[256,1024]{1,0:T(8,128)(2,1)S(1)}, u32[]{:S(2)}, u32[]{:S(2)}) collective-permute-start(bf16[256,1024]{1,0:T(8,128)(2,1)S(1)} %collective-permute-done.27), channel_id=1, source_target_pairs={{1,0},{2,1},{5,4},{6,5},{9,8},{10,9},{13,12},{14,13},{17,16},{18,1... | collective-permute-start | bytes 1572872 | tf_op jit(solution)/shard_map/ppermute | solution.py:50
  121.8 35.1 %collective-permute-start.5 = (bf16[256,1024]{1,0:T(8,128)(2,1)S(1)}, bf16[256,1024]{1,0:T(8,128)(2,1)S(1)}, u32[]{:S(2)}, u32[]{:S(2)}) collective-permute-start(bf16[256,1024]{1,0:T(8,128)(2,1)S(1)} %collective-permute-done.4), channel_id=1, source_target_pairs={{1,0},{5,4},{9,8},{13,12},{17,16},{21,20},{25,24},{29,28}} | collective-permute-start | bytes 1572872 | tf_op jit(solution)/shard_map/ppermute | solution.py:50
  124.4 71.4 %collective-permute-start.49 = (bf16[256,1024]{1,0:T(8,128)(2,1)S(1)}, bf16[256,1024]{1,0:T(8,128)(2,1)S(1)}, u32[]{:S(2)}, u32[]{:S(2)}) collective-permute-start(bf16[256,1024]{1,0:T(8,128)(2,1)S(1)} %collective-permute-done.48), channel_id=1, source_target_pairs={{1,2},{2,3},{5,6},{6,7},{9,10},{10,11},{13,14},{14,15},{17,18},{18... | collective-permute-start | bytes 1572872 | tf_op jit(solution)/shard_map/ppermute | solution.py:49
  125.1 70.8 %collective-permute-start.52 = (bf16[256,1024]{1,0:T(8,128)(2,1)S(1)}, bf16[256,1024]{1,0:T(8,128)(2,1)S(1)}, u32[]{:S(2)}, u32[]{:S(2)}) collective-permute-start(bf16[256,1024]{1,0:T(8,128)(2,1)S(1)} %collective-permute-done.51), channel_id=1, source_target_pairs={{1,0},{2,1},{5,4},{6,5},{9,8},{10,9},{13,12},{14,13},{17,16},{18,1... | collective-permute-start | bytes 1572872 | tf_op jit(solution)/shard_map/ppermute | solution.py:50
  134.5 27.7 %collective-permute-start.37 = (bf16[256,1024]{1,0:T(8,128)(2,1)S(1)}, bf16[256,1024]{1,0:T(8,128)(2,1)S(1)}, u32[]{:S(2)}, u32[]{:S(2)}) collective-permute-start(bf16[256,1024]{1,0:T(8,128)(2,1)S(1)} %collective-permute-done.36), channel_id=1, source_target_pairs={{1,2},{2,3},{5,6},{6,7},{9,10},{10,11},{13,14},{14,15},{17,18},{18... | collective-permute-start | bytes 1572872 | tf_op jit(solution)/shard_map/ppermute | solution.py:49
  145.7 50.9 %collective-permute-start.40 = (bf16[256,1024]{1,0:T(8,128)(2,1)S(1)}, bf16[256,1024]{1,0:T(8,128)(2,1)S(1)}, u32[]{:S(2)}, u32[]{:S(2)}) collective-permute-start(bf16[256,1024]{1,0:T(8,128)(2,1)S(1)} %collective-permute-done.39), channel_id=1, source_target_pairs={{1,0},{2,1},{5,4},{6,5},{9,8},{10,9},{13,12},{14,13},{17,16},{18,1... | collective-permute-start | bytes 1572872 | tf_op jit(solution)/shard_map/ppermute | solution.py:50
  157.0 32.6 %collective-permute-start.29 = (bf16[256,1024]{1,0:T(8,128)(2,1)S(1)}, bf16[256,1024]{1,0:T(8,128)(2,1)S(1)}, u32[]{:S(2)}, u32[]{:S(2)}) collective-permute-start(bf16[256,1024]{1,0:T(8,128)(2,1)S(1)} %collective-permute-done.28), channel_id=1, source_target_pairs={{1,0},{5,4},{9,8},{13,12},{17,16},{21,20},{25,24},{29,28}} | collective-permute-start | bytes 1572872 | tf_op jit(solution)/shard_map/ppermute | solution.py:50
  162.2 157.6 %collective-permute-start.17 = (bf16[512,1024]{1,0:T(8,128)(2,1)}, bf16[512,1024]{1,0:T(8,128)(2,1)}, u32[]{:S(2)}, u32[]{:S(2)}) collective-permute-start(bf16[512,1024]{1,0:T(8,128)(2,1)} %pad_maximum_fusion.2), channel_id=1, source_target_pairs={{0,4},{4,0},{8,12},{12,8},{16,20},{20,16},{24,28},{28,24},{1,5},{5... | collective-permute-start | bytes 3145736 | tf_op jit(solution)/shard_map/ppermute | solution.py:90
  195.8 123.9 %collective-permute-start.14 = (bf16[512,1024]{1,0:T(8,128)(2,1)}, bf16[512,1024]{1,0:T(8,128)(2,1)}, u32[]{:S(2)}, u32[]{:S(2)}) collective-permute-start(bf16[512,1024]{1,0:T(8,128)(2,1)} %pad_maximum_fusion.1), channel_id=1, source_target_pairs={{0,4},{4,0},{8,12},{12,8},{16,20},{20,16},{24,28},{28,24},{1,5},{5... | collective-permute-start | bytes 3145736 | tf_op jit(solution)/shard_map/ppermute | solution.py:90
  196.6 16.6 %collective-permute-start.53 = (bf16[256,1024]{1,0:T(8,128)(2,1)S(1)}, bf16[256,1024]{1,0:T(8,128)(2,1)S(1)}, u32[]{:S(2)}, u32[]{:S(2)}) collective-permute-start(bf16[256,1024]{1,0:T(8,128)(2,1)S(1)} %collective-permute-done.52), channel_id=1, source_target_pairs={{1,0},{5,4},{9,8},{13,12},{17,16},{21,20},{25,24},{29,28}} | collective-permute-start | bytes 1572872 | tf_op jit(solution)/shard_map/ppermute | solution.py:50
  197.9 29.0 %collective-permute-start.41 = (bf16[256,1024]{1,0:T(8,128)(2,1)S(1)}, bf16[256,1024]{1,0:T(8,128)(2,1)S(1)}, u32[]{:S(2)}, u32[]{:S(2)}) collective-permute-start(bf16[256,1024]{1,0:T(8,128)(2,1)S(1)} %collective-permute-done.40), channel_id=1, source_target_pairs={{1,0},{5,4},{9,8},{13,12},{17,16},{21,20},{25,24},{29,28}} | collective-permute-start | bytes 1572872 | tf_op jit(solution)/shard_map/ppermute | solution.py:50
  290.8 26.9 %collective-permute-start.63 = (bf16[2,2,1,128,256]{4,3,2,1,0:T(8,128)(2,1)}, bf16[2,2,1,128,256]{4,3,2,1,0:T(8,128)(2,1)S(1)}, u32[]{:S(2)}, u32[]{:S(2)}) collective-permute-start(bf16[2,2,1,128,256]{4,3,2,1,0:T(8,128)(2,1)} %dynamic-slice_convert_fusion.16), channel_id=1, source_target_pairs={{0,4},{4,0},{8,12},{12,8},{16,20},{20,16},{24,28},{28,24},{1,5},{5... | collective-permute-start | bytes 786440 | tf_op jit(solution)/shard_map/ppermute | solution.py:115
  304.2 109.0 %collective-permute-start.60 = (bf16[2,2,1,128,768]{4,3,2,1,0:T(8,128)(2,1)}, bf16[2,2,1,128,768]{4,3,2,1,0:T(8,128)(2,1)}, u32[]{:S(2)}, u32[]{:S(2)}) collective-permute-start(bf16[2,2,1,128,768]{4,3,2,1,0:T(8,128)(2,1)} %dynamic-slice_convert_fusion.2), channel_id=1, source_target_pairs={{0,4},{4,0},{8,12},{12,8},{16,20},{20,16},{24,28},{28,24},{1,5},{5... | collective-permute-start | bytes 2359304 | tf_op jit(solution)/shard_map/ppermute | solution.py:115
  317.8 89.0 %collective-permute-start.64 = (bf16[1,2,1,128,256]{4,3,2,1,0:T(8,128)(2,1)S(1)}, bf16[1,2,1,128,256]{4,3,2,1,0:T(8,128)(2,1)S(1)}, u32[]{:S(2)}, u32[]{:S(2)}) collective-permute-start(bf16[1,2,1,128,256]{4,3,2,1,0:T(8,128)(2,1)S(1)} %dynamic-slice_convert_fusion.18), channel_id=1, source_target_pairs={{0,16},{4,20},{8,24},{12,28},{16,0},{20,4},{24,8},{28,12},{1,17},{... | collective-permute-start | bytes 393224 | tf_op jit(solution)/shard_map/ppermute | solution.py:115
  377.5 69.3 %collective-permute-start.66 = (bf16[2,2,1,128,1024]{4,3,2,1,0:T(8,128)(2,1)}, bf16[2,2,1,128,1024]{4,3,2,1,0:T(8,128)(2,1)}, u32[]{:S(2)}, u32[]{:S(2)}) collective-permute-start(bf16[2,2,1,128,1024]{4,3,2,1,0:T(8,128)(2,1)} %dynamic-slice_convert_fusion.1), channel_id=1, source_target_pairs={{0,4},{4,0},{8,12},{12,8},{16,20},{20,16},{24,28},{28,24},{1,5},{5... | collective-permute-start | bytes 3145736 | tf_op jit(solution)/shard_map/ppermute | solution.py:115
  385.3 67.5 %collective-permute-start.69 = (bf16[2,2,1,128,1024]{4,3,2,1,0:T(8,128)(2,1)}, bf16[2,2,1,128,1024]{4,3,2,1,0:T(8,128)(2,1)}, u32[]{:S(2)}, u32[]{:S(2)}) collective-permute-start(bf16[2,2,1,128,1024]{4,3,2,1,0:T(8,128)(2,1)} %dynamic-slice_convert_fusion), channel_id=1, source_target_pairs={{0,4},{4,0},{8,12},{12,8},{16,20},{20,16},{24,28},{28,24},{1,5},{5... | collective-permute-start | bytes 3145736 | tf_op jit(solution)/shard_map/ppermute | solution.py:115
  387.8 28.2 %collective-permute-start.18 = (bf16[256,1024]{1,0:T(8,128)(2,1)}, bf16[256,1024]{1,0:T(8,128)(2,1)}, u32[]{:S(2)}, u32[]{:S(2)}) collective-permute-start(bf16[256,1024]{1,0:T(8,128)(2,1)} %get-tuple-element.183), channel_id=1, source_target_pairs={{0,1},{4,5},{8,9},{12,13},{16,17},{20,21},{24,25},{28,29}} | collective-permute-start | bytes 1572872 | tf_op jit(solution)/shard_map/ppermute | solution.py:73
  411.2 13.7 %collective-permute-start.30 = (bf16[256,1024]{1,0:T(8,128)(2,1)S(1)}, bf16[256,1024]{1,0:T(8,128)(2,1)S(1)}, u32[]{:S(2)}, u32[]{:S(2)}) collective-permute-start(bf16[256,1024]{1,0:T(8,128)(2,1)S(1)} %copy-done.61), channel_id=1, source_target_pairs={{0,1},{4,5},{8,9},{12,13},{16,17},{20,21},{24,25},{28,29}} | collective-permute-start | bytes 1572872 | tf_op jit(solution)/shard_map/ppermute | solution.py:73
  413.2 22.9 %collective-permute-start.54 = (bf16[256,1024]{1,0:T(8,128)(2,1)S(1)}, bf16[256,1024]{1,0:T(8,128)(2,1)S(1)}, u32[]{:S(2)}, u32[]{:S(2)}) collective-permute-start(bf16[256,1024]{1,0:T(8,128)(2,1)S(1)} %get-tuple-element.175), channel_id=1, source_target_pairs={{0,1},{4,5},{8,9},{12,13},{16,17},{20,21},{24,25},{28,29}} | collective-permute-start | bytes 1572872 | tf_op jit(solution)/shard_map/ppermute | solution.py:73
  415.9 29.2 %collective-permute-start.42 = (bf16[256,1024]{1,0:T(8,128)(2,1)S(1)}, bf16[256,1024]{1,0:T(8,128)(2,1)S(1)}, u32[]{:S(2)}, u32[]{:S(2)}) collective-permute-start(bf16[256,1024]{1,0:T(8,128)(2,1)S(1)} %get-tuple-element.179), channel_id=1, source_target_pairs={{0,1},{4,5},{8,9},{12,13},{16,17},{20,21},{24,25},{28,29}} | collective-permute-start | bytes 1572872 | tf_op jit(solution)/shard_map/ppermute | solution.py:73
  424.8 31.7 %collective-permute-start.21 = (bf16[256,1024]{1,0:T(8,128)(2,1)S(1)}, bf16[256,1024]{1,0:T(8,128)(2,1)S(1)}, u32[]{:S(2)}, u32[]{:S(2)}) collective-permute-start(bf16[256,1024]{1,0:T(8,128)(2,1)S(1)} %copy-done.60), channel_id=1, source_target_pairs={{3,2},{7,6},{11,10},{15,14},{19,18},{23,22},{27,26},{31,30}} | collective-permute-start | bytes 1572872 | tf_op jit(solution)/shard_map/ppermute | solution.py:74
  445.1 23.3 %collective-permute-start.33 = (bf16[256,1024]{1,0:T(8,128)(2,1)S(1)}, bf16[256,1024]{1,0:T(8,128)(2,1)S(1)}, u32[]{:S(2)}, u32[]{:S(2)}) collective-permute-start(bf16[256,1024]{1,0:T(8,128)(2,1)S(1)} %copy-done.59), channel_id=1, source_target_pairs={{3,2},{7,6},{11,10},{15,14},{19,18},{23,22},{27,26},{31,30}} | collective-permute-start | bytes 1572872 | tf_op jit(solution)/shard_map/ppermute | solution.py:74
  446.0 29.8 %collective-permute-start.57 = (bf16[256,1024]{1,0:T(8,128)(2,1)S(1)}, bf16[256,1024]{1,0:T(8,128)(2,1)S(1)}, u32[]{:S(2)}, u32[]{:S(2)}) collective-permute-start(bf16[256,1024]{1,0:T(8,128)(2,1)S(1)} %get-tuple-element.176), channel_id=1, source_target_pairs={{3,2},{7,6},{11,10},{15,14},{19,18},{23,22},{27,26},{31,30}} | collective-permute-start | bytes 1572872 | tf_op jit(solution)/shard_map/ppermute | solution.py:74
  446.8 16.8 %collective-permute-start.19 = (bf16[256,1024]{1,0:T(8,128)(2,1)S(1)}, bf16[256,1024]{1,0:T(8,128)(2,1)S(1)}, u32[]{:S(2)}, u32[]{:S(2)}) collective-permute-start(bf16[256,1024]{1,0:T(8,128)(2,1)S(1)} %add_convert_fusion.15), channel_id=1, source_target_pairs={{0,1},{1,2},{4,5},{5,6},{8,9},{9,10},{12,13},{13,14},{16,17},{17,1... | collective-permute-start | bytes 1572872 | tf_op jit(solution)/shard_map/ppermute | solution.py:73
  452.9 22.0 %collective-permute-start.31 = (bf16[256,1024]{1,0:T(8,128)(2,1)S(1)}, bf16[256,1024]{1,0:T(8,128)(2,1)S(1)}, u32[]{:S(2)}, u32[]{:S(2)}) collective-permute-start(bf16[256,1024]{1,0:T(8,128)(2,1)S(1)} %add_convert_fusion.11), channel_id=1, source_target_pairs={{0,1},{1,2},{4,5},{5,6},{8,9},{9,10},{12,13},{13,14},{16,17},{17,1... | collective-permute-start | bytes 1572872 | tf_op jit(solution)/shard_map/ppermute | solution.py:73
  456.5 34.3 %collective-permute-start.45 = (bf16[256,1024]{1,0:T(8,128)(2,1)S(1)}, bf16[256,1024]{1,0:T(8,128)(2,1)S(1)}, u32[]{:S(2)}, u32[]{:S(2)}) collective-permute-start(bf16[256,1024]{1,0:T(8,128)(2,1)S(1)} %get-tuple-element.180), channel_id=1, source_target_pairs={{3,2},{7,6},{11,10},{15,14},{19,18},{23,22},{27,26},{31,30}} | collective-permute-start | bytes 1572872 | tf_op jit(solution)/shard_map/ppermute | solution.py:74
  463.6 22.5 %collective-permute-start.55 = (bf16[256,1024]{1,0:T(8,128)(2,1)S(1)}, bf16[256,1024]{1,0:T(8,128)(2,1)S(1)}, u32[]{:S(2)}, u32[]{:S(2)}) collective-permute-start(bf16[256,1024]{1,0:T(8,128)(2,1)S(1)} %add_convert_fusion.3), channel_id=1, source_target_pairs={{0,1},{1,2},{4,5},{5,6},{8,9},{9,10},{12,13},{13,14},{16,17},{17,1... | collective-permute-start | bytes 1572872 | tf_op jit(solution)/shard_map/ppermute | solution.py:73
  468.4 28.9 %collective-permute-start.43 = (bf16[256,1024]{1,0:T(8,128)(2,1)S(1)}, bf16[256,1024]{1,0:T(8,128)(2,1)S(1)}, u32[]{:S(2)}, u32[]{:S(2)}) collective-permute-start(bf16[256,1024]{1,0:T(8,128)(2,1)S(1)} %add_convert_fusion.7), channel_id=1, source_target_pairs={{0,1},{1,2},{4,5},{5,6},{8,9},{9,10},{12,13},{13,14},{16,17},{17,1... | collective-permute-start | bytes 1572872 | tf_op jit(solution)/shard_map/ppermute | solution.py:73
  474.8 23.8 %collective-permute-start.67 = (bf16[1,2,1,128,1024]{4,3,2,1,0:T(8,128)(2,1)S(1)}, bf16[1,2,1,128,1024]{4,3,2,1,0:T(8,128)(2,1)S(1)}, u32[]{:S(2)}, u32[]{:S(2)}) collective-permute-start(bf16[1,2,1,128,1024]{4,3,2,1,0:T(8,128)(2,1)S(1)} %dynamic-slice_convert_fusion.4), channel_id=1, source_target_pairs={{0,16},{4,20},{8,24},{12,28},{16,0},{20,4},{24,8},{28,12},{1,17},{... | collective-permute-start | bytes 1572872 | tf_op jit(solution)/shard_map/ppermute | solution.py:115
  475.8 23.7 %collective-permute-start.70 = (bf16[2,1,1,128,1024]{4,3,2,1,0:T(8,128)(2,1)S(1)}, bf16[2,1,1,128,1024]{4,3,2,1,0:T(8,128)(2,1)S(1)}, u32[]{:S(2)}, u32[]{:S(2)}) collective-permute-start(bf16[2,1,1,128,1024]{4,3,2,1,0:T(8,128)(2,1)S(1)} %dynamic-slice_convert_fusion.3), channel_id=1, source_target_pairs={{0,8},{4,12},{8,0},{12,4},{16,24},{20,28},{24,16},{28,20},{1,9},{5... | collective-permute-start | bytes 1572872 | tf_op jit(solution)/shard_map/ppermute | solution.py:115
  486.1 55.4 %collective-permute-start.20 = (bf16[256,1024]{1,0:T(8,128)(2,1)S(1)}, bf16[256,1024]{1,0:T(8,128)(2,1)S(1)}, u32[]{:S(2)}, u32[]{:S(2)}) collective-permute-start(bf16[256,1024]{1,0:T(8,128)(2,1)S(1)} %get-tuple-element.181), channel_id=1, source_target_pairs={{0,1},{1,2},{2,3},{4,5},{5,6},{6,7},{8,9},{9,10},{10,11},{12,13},{... | collective-permute-start | bytes 1572872 | tf_op jit(solution)/shard_map/ppermute | solution.py:73
  490.9 39.4 %collective-permute-start.22 = (bf16[256,1024]{1,0:T(8,128)(2,1)S(1)}, bf16[256,1024]{1,0:T(8,128)(2,1)S(1)}, u32[]{:S(2)}, u32[]{:S(2)}) collective-permute-start(bf16[256,1024]{1,0:T(8,128)(2,1)S(1)} %get-tuple-element.182), channel_id=1, source_target_pairs={{2,1},{3,2},{6,5},{7,6},{10,9},{11,10},{14,13},{15,14},{18,17},{19... | collective-permute-start | bytes 1572872 | tf_op jit(solution)/shard_map/ppermute | solution.py:74
  497.3 34.7 %collective-permute-start.34 = (bf16[256,1024]{1,0:T(8,128)(2,1)S(1)}, bf16[256,1024]{1,0:T(8,128)(2,1)S(1)}, u32[]{:S(2)}, u32[]{:S(2)}) collective-permute-start(bf16[256,1024]{1,0:T(8,128)(2,1)S(1)} %get-tuple-element.186), channel_id=1, source_target_pairs={{2,1},{3,2},{6,5},{7,6},{10,9},{11,10},{14,13},{15,14},{18,17},{19... | collective-permute-start | bytes 1572872 | tf_op jit(solution)/shard_map/ppermute | solution.py:74
  499.5 37.3 %collective-permute-start.58 = (bf16[256,1024]{1,0:T(8,128)(2,1)S(1)}, bf16[256,1024]{1,0:T(8,128)(2,1)S(1)}, u32[]{:S(2)}, u32[]{:S(2)}) collective-permute-start(bf16[256,1024]{1,0:T(8,128)(2,1)S(1)} %get-tuple-element.174), channel_id=1, source_target_pairs={{2,1},{3,2},{6,5},{7,6},{10,9},{11,10},{14,13},{15,14},{18,17},{19... | collective-permute-start | bytes 1572872 | tf_op jit(solution)/shard_map/ppermute | solution.py:74
  500.4 42.4 %collective-permute-start.44 = (bf16[256,1024]{1,0:T(8,128)(2,1)S(1)}, bf16[256,1024]{1,0:T(8,128)(2,1)S(1)}, u32[]{:S(2)}, u32[]{:S(2)}) collective-permute-start(bf16[256,1024]{1,0:T(8,128)(2,1)S(1)} %get-tuple-element.177), channel_id=1, source_target_pairs={{0,1},{1,2},{2,3},{4,5},{5,6},{6,7},{8,9},{9,10},{10,11},{12,13},{... | collective-permute-start | bytes 1572872 | tf_op jit(solution)/shard_map/ppermute | solution.py:73
  530.3 14.3 %collective-permute-start.47 = (bf16[256,1024]{1,0:T(8,128)(2,1)S(1)}, bf16[256,1024]{1,0:T(8,128)(2,1)S(1)}, u32[]{:S(2)}, u32[]{:S(2)}) collective-permute-start(bf16[256,1024]{1,0:T(8,128)(2,1)S(1)} %add_convert_fusion.4), channel_id=1, source_target_pairs={{1,0},{2,1},{3,2},{5,4},{6,5},{7,6},{9,8},{10,9},{11,10},{13,12},{... | collective-permute-start | bytes 1572872 | tf_op jit(solution)/shard_map/ppermute | solution.py:74
  532.0 19.3 %collective-permute-start.32 = (bf16[256,1024]{1,0:T(8,128)(2,1)S(1)}, bf16[256,1024]{1,0:T(8,128)(2,1)S(1)}, u32[]{:S(2)}, u32[]{:S(2)}) collective-permute-start(bf16[256,1024]{1,0:T(8,128)(2,1)S(1)} %get-tuple-element.185), channel_id=1, source_target_pairs={{0,1},{1,2},{2,3},{4,5},{5,6},{6,7},{8,9},{9,10},{10,11},{12,13},{... | collective-permute-start | bytes 1572872 | tf_op jit(solution)/shard_map/ppermute | solution.py:73
  536.8 20.1 %collective-permute-start.56 = (bf16[256,1024]{1,0:T(8,128)(2,1)S(1)}, bf16[256,1024]{1,0:T(8,128)(2,1)S(1)}, u32[]{:S(2)}, u32[]{:S(2)}) collective-permute-start(bf16[256,1024]{1,0:T(8,128)(2,1)S(1)} %get-tuple-element.173), channel_id=1, source_target_pairs={{0,1},{1,2},{2,3},{4,5},{5,6},{6,7},{8,9},{9,10},{10,11},{12,13},{... | collective-permute-start | bytes 1572872 | tf_op jit(solution)/shard_map/ppermute | solution.py:73
  541.5 16.9 %collective-permute-start.23 = (bf16[256,1024]{1,0:T(8,128)(2,1)S(1)}, bf16[256,1024]{1,0:T(8,128)(2,1)S(1)}, u32[]{:S(2)}, u32[]{:S(2)}) collective-permute-start(bf16[256,1024]{1,0:T(8,128)(2,1)S(1)} %add_convert_fusion.12), channel_id=1, source_target_pairs={{1,0},{2,1},{3,2},{5,4},{6,5},{7,6},{9,8},{10,9},{11,10},{13,12},{... | collective-permute-start | bytes 1572872 | tf_op jit(solution)/shard_map/ppermute | solution.py:74
  542.8 26.7 %collective-permute-start.35 = (bf16[256,1024]{1,0:T(8,128)(2,1)S(1)}, bf16[256,1024]{1,0:T(8,128)(2,1)S(1)}, u32[]{:S(2)}, u32[]{:S(2)}) collective-permute-start(bf16[256,1024]{1,0:T(8,128)(2,1)S(1)} %add_convert_fusion.8), channel_id=1, source_target_pairs={{1,0},{2,1},{3,2},{5,4},{6,5},{7,6},{9,8},{10,9},{11,10},{13,12},{... | collective-permute-start | bytes 1572872 | tf_op jit(solution)/shard_map/ppermute | solution.py:74
  544.5 30.6 %collective-permute-start.59 = (bf16[256,1024]{1,0:T(8,128)(2,1)S(1)}, bf16[256,1024]{1,0:T(8,128)(2,1)S(1)}, u32[]{:S(2)}, u32[]{:S(2)}) collective-permute-start(bf16[256,1024]{1,0:T(8,128)(2,1)S(1)} %add_convert_fusion), channel_id=1, source_target_pairs={{1,0},{2,1},{3,2},{5,4},{6,5},{7,6},{9,8},{10,9},{11,10},{13,12},{... | collective-permute-start | bytes 1572872 | tf_op jit(solution)/shard_map/ppermute | solution.py:74
  551.3 26.0 %collective-permute-start.62 = (bf16[1,1,1,128,768]{4,3,2,1,0:T(8,128)(2,1)S(1)}, bf16[1,1,1,128,768]{4,3,2,1,0:T(8,128)(2,1)S(1)}, u32[]{:S(2)}, u32[]{:S(2)}) collective-permute-start(bf16[1,1,1,128,768]{4,3,2,1,0:T(8,128)(2,1)S(1)} %dynamic-slice_convert_fusion.17), channel_id=1, source_target_pairs={{0,16},{4,20},{8,24},{12,28},{16,0},{20,4},{24,8},{28,12},{1,17},{... | collective-permute-start | bytes 589832 | tf_op jit(solution)/shard_map/ppermute | solution.py:115
  556.9 23.1 %collective-permute-start.68 = (bf16[1,1,1,128,1024]{4,3,2,1,0:T(8,128)(2,1)S(1)}, bf16[1,1,1,128,1024]{4,3,2,1,0:T(8,128)(2,1)S(1)}, u32[]{:S(2)}, u32[]{:S(2)}) collective-permute-start(bf16[1,1,1,128,1024]{4,3,2,1,0:T(8,128)(2,1)S(1)} %dynamic-slice_convert_fusion.15), channel_id=1, source_target_pairs={{0,8},{4,12},{8,0},{12,4},{16,24},{20,28},{24,16},{28,20},{1,9},{5... | collective-permute-start | bytes 786440 | tf_op jit(solution)/shard_map/ppermute | solution.py:115
  558.4 24.6 %collective-permute-start.71 = (bf16[1,1,1,128,1024]{4,3,2,1,0:T(8,128)(2,1)S(1)}, bf16[1,1,1,128,1024]{4,3,2,1,0:T(8,128)(2,1)S(1)}, u32[]{:S(2)}, u32[]{:S(2)}) collective-permute-start(bf16[1,1,1,128,1024]{4,3,2,1,0:T(8,128)(2,1)S(1)} %dynamic-slice_convert_fusion.14), channel_id=1, source_target_pairs={{0,16},{4,20},{8,24},{12,28},{16,0},{20,4},{24,8},{28,12},{1,17},{... | collective-permute-start | bytes 786440 | tf_op jit(solution)/shard_map/ppermute | solution.py:115
  (114 other events, 1376.3 us)
